TPU v7x, 1024 devices: a whole 4x4x32 slice. The times are simulated.
1024 devices in a mesh: dp: 8 (over y, core), expert: 32 (over x, z_lo), hid: 4 (over z_hi).
Axes of the slice: x: 4, y: 4, z: 32 (z_hi: 4, z_lo: 8; z = z_hi * 8 + z_lo), core: 2. Of those that a mesh axis runs over, the one named last changes fastest.
Arguments:
- images_in: bfloat16 [1024, 256, 1024], P(('dp', 'expert', 'hid')), may hold values from -16 to 16
- slot_keys: bfloat16 [1024, 128], replicated, may hold values from -6 to 6
- w_in: bfloat16 [64, 1024, 4096], P('expert', None, 'hid'), may hold values from -0.1875 to 0.1875
- w_out: bfloat16 [64, 4096, 1024], P('expert', 'hid'), may hold values from -0.09375 to 0.09375
Outputs:
- mixed: bfloat16 [1024, 256, 1024], P(('dp', 'expert', 'hid'))
All inputs are finite; a program needn't handle non-finite values.
Results may differ from a plain program's by a relative error of at most 0.013.
Values may be sent and summed in bfloat16 or wider, within the bound.
No kernel may reach another device: no remote copies, remote signals or barrier semaphores. Data moves between devices by JAX's collectives and lax.ppermute only.
A program may use at most 32 MiB of HBM per device.

v0:
```python
import jax
import jax.numpy as jnp
from jax import lax
from jax.sharding import PartitionSpec as P

SLOTS = 2


def normal_rows(values):
    floats = values.astype(jnp.float32)
    return (floats * lax.rsqrt(jnp.mean(floats * floats, axis=-1, keepdims=True) + 1e-06)).astype(
        jnp.bfloat16
    )


def unit_columns(values):
    floats = values.astype(jnp.float32)
    return (floats * lax.rsqrt(jnp.sum(floats * floats, axis=0, keepdims=True) + 1e-06)).astype(
        jnp.bfloat16
    )


def swap(value, masks):
    groups, ring = lax.axis_size("dp"), lax.axis_size("hid")
    pairs = [
        (group * ring + i, group * ring + (i ^ masks[group % 2]))
        for group in range(groups)
        for i in range(ring)
    ]
    return lax.ppermute(value, ("dp", "hid"), pairs)


def near(value):
    return swap(value, (1, 3))


def far(value):
    return swap(value, (3, 1))


def expert(rows, w_in, w_out):
    hidden = jax.nn.gelu(
        jnp.dot(rows, w_in, preferred_element_type=jnp.float32), approximate=True
    ).astype(jnp.bfloat16)
    return jnp.dot(hidden, w_out, preferred_element_type=jnp.float32)


def exchange(own, w_in, w_out):
    count = own.shape[0]
    beside = near(own)
    pair = jnp.concatenate([own, beside])
    others = far(pair)
    others, here = lax.optimization_barrier((others, expert(pair, w_in, w_out)))
    there = expert(others, w_in, w_out).astype(jnp.bfloat16)
    back = far(there)
    total = here + back.astype(jnp.float32)
    total, rest = total[:count], total[count:].astype(jnp.bfloat16)
    rest = near(rest)
    return (total + rest.astype(jnp.float32)).astype(jnp.bfloat16)


def layer(images_in, slot_keys, w_in, w_out):
    unit_keys = unit_columns(slot_keys)
    normed = normal_rows(images_in)
    logits = 2.0 * jnp.einsum("itd,de->ite", normed, unit_keys, preferred_element_type=jnp.float32)
    powers = jnp.exp(logits)
    dispatch = (powers / jnp.sum(powers, axis=1, keepdims=True)).astype(jnp.bfloat16)
    combine = (powers / jnp.sum(powers, axis=2, keepdims=True)).astype(jnp.bfloat16)
    slot_in = jnp.einsum(
        "ite,itd->ied", dispatch, images_in, preferred_element_type=jnp.float32
    ).astype(jnp.bfloat16)
    owners = lax.axis_size("expert")
    local_experts = w_in.shape[0]
    d_width = w_in.shape[1]
    grouped = slot_in.reshape(owners, local_experts, SLOTS, d_width)
    arrived = lax.all_to_all(grouped, "expert", 0, 0, tiled=True)
    results = []
    for b in range(local_experts):
        own = arrived[:, b].reshape(-1, d_width)
        results.append(exchange(own, w_in[b], w_out[b]).reshape(owners, SLOTS, d_width))
    results = lax.all_to_all(jnp.stack(results, axis=1), "expert", 0, 0, tiled=True)
    results = results.reshape(1, -1, d_width)
    return jnp.einsum("ite,ied->itd", combine, results, preferred_element_type=jnp.float32).astype(
        jnp.bfloat16
    )


def solution(mesh):
    return jax.shard_map(
        layer,
        mesh=mesh,
        in_specs=(
            P(("dp", "expert", "hid"), None, None),
            P(),
            P("expert", None, "hid"),
            P("expert", "hid", None),
        ),
        out_specs=P(("dp", "expert", "hid"), None, None),
        check_vma=False,
    )
```

profile of v0, /device:TPU:24, one launch (start us, length us, event | category | flops | bytes accessed | tf_op | source)
XLA Modules:
  0.0 238.4 jit_solution(8855470128226793741)
XLA Ops:
  0.0 1.2 fusion.32
  1.2 1.1 fusion.34
  2.3 1.6 fusion.134
  3.9 1.3 convolution_convert_fusion.1
  5.3 34.7 %all_to_all.10 = bf16[32,2,2,1024]{3,2,1,0:T(2,128)(2,1)S(1)} all-to-all(bf16[32,2,2,1024]{3,2,1,0:T(2,128)(2,1)S(1)} %reshape.61), channel_id=1, replica_groups=mesh['dp'=8,'expert'=32,'hid'=4] {'expert'}, dimensions={0} | all-to-all | bytes 524288 | tf_op jit(solution)/shard_map/all_to_all | solution.py:76
  40.3 15.7 %collective-permute-start = (bf16[64,1024]{1,0:T(8,128)(2,1)S(1)}, bf16[64,1024]{1,0:T(8,128)(2,1)S(1)}, u32[]{:S(2)}, u32[]{:S(2)}) collective-permute-start(bf16[64,1024]{1,0:T(8,128)(2,1)S(1)} %reshape_squeeze.6), channel_id=1, source_target_pairs={{0,1},{1,0},{2,3},{3,2},{128,131},{129,130},{130,129},{131,128},{2... | collective-permute-start | bytes 393224 | tf_op jit(solution)/shard_map/ppermute | solution.py:30
  56.1 1.9 collective-permute-start.4
  58.0 10.1 %collective-permute-done = bf16[64,1024]{1,0:T(8,128)(2,1)S(1)} collective-permute-done((bf16[64,1024]{1,0:T(8,128)(2,1)S(1)}, bf16[64,1024]{1,0:T(8,128)(2,1)S(1)}, u32[]{:S(2)}, u32[]{:S(2)}) %collective-permute-start) | collective-permute-done | bytes 131104 | tf_op jit(solution)/shard_map/ppermute | solution.py:30
  68.1 17.9 %collective-permute-start.1 = (bf16[128,1024]{1,0:T(8,128)(2,1)S(1)}, bf16[128,1024]{1,0:T(8,128)(2,1)S(1)}, u32[]{:S(2)}, u32[]{:S(2)}) collective-permute-start(bf16[128,1024]{1,0:T(8,128)(2,1)S(1)} %constant_dynamic-update-slice_fusion), channel_id=1, source_target_pairs={{0,3},{1,2},{2,1},{3,0},{128,129},{129,128},{130,131},{131,130},{2... | collective-permute-start | bytes 786440 | tf_op jit(solution)/shard_map/ppermute | solution.py:30
  86.1 1.9 collective-permute-start.5
  88.0 3.1 %fusion.10 = f32[128,1024]{1,0:T(8,128)S(1)} fusion(bf16[2,1024,1024]{2,1,0:T(8,128)(2,1)} %param.7, bf16[128,1024]{1,0:T(8,128)(2,1)S(1)} %constant_dynamic-update-slice_fusion, bf16[2,1024,1024]{2,1,0:T(8,128)(2,1)} %param.6), kind=kOutput, calls=%fused_computation.10 | convolution fusion | flops 538050560 | bytes 4980736 | tf_op jit(solution)/shard_map/dot_general | solution.py:45
  91.1 3.1 %fusion.2 = f32[128,1024]{1,0:T(8,128)S(1)} fusion(bf16[2,1024,1024]{2,1,0:T(8,128)(2,1)} %param.7, bf16[128,1024]{1,0:T(8,128)(2,1)S(1)} %constant_dynamic-update-slice_fusion.2, bf16[2,1024,1024]{2,1,0:T(8,128)(2,1)} %param.6), kind=kOutput, calls=%fused_computation.2 | convolution fusion | flops 538050560 | bytes 4980736 | tf_op jit(solution)/shard_map/dot_general | solution.py:45
  94.2 26.4 %collective-permute-done.1 = bf16[128,1024]{1,0:T(8,128)(2,1)S(1)} collective-permute-done((bf16[128,1024]{1,0:T(8,128)(2,1)S(1)}, bf16[128,1024]{1,0:T(8,128)(2,1)S(1)}, u32[]{:S(2)}, u32[]{:S(2)}) %collective-permute-start.1) | collective-permute-done | bytes 262176 | tf_op jit(solution)/shard_map/ppermute | solution.py:30
  120.6 3.1 %fusion.25 = bf16[128,1024]{1,0:T(8,128)(2,1)S(1)} fusion(bf16[2,1024,1024]{2,1,0:T(8,128)(2,1)} %param.7, bf16[128,1024]{1,0:T(8,128)(2,1)S(1)} %collective-permute-done.1, bf16[2,1024,1024]{2,1,0:T(8,128)(2,1)} %param.6), kind=kOutput, calls=%fused_computation.28 | convolution fusion | flops 538181632 | bytes 4718592 | tf_op jit(solution)/shard_map/dot_general | solution.py:45
  123.7 11.0 %collective-permute-start.2 = (bf16[128,1024]{1,0:T(8,128)(2,1)S(1)}, bf16[128,1024]{1,0:T(8,128)(2,1)S(1)}, u32[]{:S(2)}, u32[]{:S(2)}) collective-permute-start(bf16[128,1024]{1,0:T(8,128)(2,1)S(1)} %fusion.25), channel_id=1, source_target_pairs={{0,3},{1,2},{2,1},{3,0},{128,129},{129,128},{130,131},{131,130},{2... | collective-permute-start | bytes 786440 | tf_op jit(solution)/shard_map/ppermute | solution.py:30
  134.7 3.1 %fusion.28 = bf16[128,1024]{1,0:T(8,128)(2,1)S(1)} fusion(bf16[2,1024,1024]{2,1,0:T(8,128)(2,1)} %param.7, bf16[128,1024]{1,0:T(8,128)(2,1)S(1)} %collective-permute-done.5, bf16[2,1024,1024]{2,1,0:T(8,128)(2,1)} %param.6), kind=kOutput, calls=%fused_computation.29 | convolution fusion | flops 538181632 | bytes 4718592 | tf_op jit(solution)/shard_map/dot_general | solution.py:45
  137.8 3.6 %collective-permute-start.6 = (bf16[128,1024]{1,0:T(8,128)(2,1)S(1)}, bf16[128,1024]{1,0:T(8,128)(2,1)S(1)}, u32[]{:S(2)}, u32[]{:S(2)}) collective-permute-start(bf16[128,1024]{1,0:T(8,128)(2,1)S(1)} %fusion.28), channel_id=1, source_target_pairs={{0,3},{1,2},{2,1},{3,0},{128,129},{129,128},{130,131},{131,130},{2... | collective-permute-start | bytes 786440 | tf_op jit(solution)/shard_map/ppermute | solution.py:30
  141.4 30.4 %collective-permute-done.2 = bf16[128,1024]{1,0:T(8,128)(2,1)S(1)} collective-permute-done((bf16[128,1024]{1,0:T(8,128)(2,1)S(1)}, bf16[128,1024]{1,0:T(8,128)(2,1)S(1)}, u32[]{:S(2)}, u32[]{:S(2)}) %collective-permute-start.2) | collective-permute-done | bytes 262176 | tf_op jit(solution)/shard_map/ppermute | solution.py:30
  171.9 8.2 %collective-permute-start.3 = (bf16[64,1024]{1,0:T(8,128)(2,1)S(1)}, bf16[64,1024]{1,0:T(8,128)(2,1)S(1)}, u32[]{:S(2)}, u32[]{:S(2)}) collective-permute-start(bf16[64,1024]{1,0:T(8,128)(2,1)S(1)} %slice.117), channel_id=1, source_target_pairs={{0,1},{1,0},{2,3},{3,2},{128,131},{129,130},{130,129},{131,128},{2... | collective-permute-start | bytes 393224 | tf_op jit(solution)/shard_map/ppermute | solution.py:30
  180.2 6.3 %collective-permute-start.7 = (bf16[64,1024]{1,0:T(8,128)(2,1)S(1)}, bf16[64,1024]{1,0:T(8,128)(2,1)S(1)}, u32[]{:S(2)}, u32[]{:S(2)}) collective-permute-start(bf16[64,1024]{1,0:T(8,128)(2,1)S(1)} %slice.116), channel_id=1, source_target_pairs={{0,1},{1,0},{2,3},{3,2},{128,131},{129,130},{130,129},{131,128},{2... | collective-permute-start | bytes 393224 | tf_op jit(solution)/shard_map/ppermute | solution.py:30
  186.6 9.9 %collective-permute-done.3 = bf16[64,1024]{1,0:T(8,128)(2,1)S(1)} collective-permute-done((bf16[64,1024]{1,0:T(8,128)(2,1)S(1)}, bf16[64,1024]{1,0:T(8,128)(2,1)S(1)}, u32[]{:S(2)}, u32[]{:S(2)}) %collective-permute-start.3) | collective-permute-done | bytes 131104 | tf_op jit(solution)/shard_map/ppermute | solution.py:30
  196.5 1.4 collective-permute-done.7
  198.4 38.7 %all_to_all.11 = bf16[32,2,2,1024]{3,2,1,0:T(2,128)(2,1)S(1)} all-to-all(bf16[32,2,2,1024]{3,2,1,0:T(2,128)(2,1)S(1)} %pad_maximum_fusion), channel_id=1, replica_groups=mesh['dp'=8,'expert'=32,'hid'=4] {'expert'}, dimensions={0} | all-to-all | bytes 524288 | tf_op jit(solution)/shard_map/all_to_all | solution.py:81
  237.2 1.1 fusion.24
  (23 shorter events, 1.2 us)
Async XLA Ops:
  40.3 27.8 %collective-permute-start = (bf16[64,1024]{1,0:T(8,128)(2,1)S(1)}, bf16[64,1024]{1,0:T(8,128)(2,1)S(1)}, u32[]{:S(2)}, u32[]{:S(2)}) collective-permute-start(bf16[64,1024]{1,0:T(8,128)(2,1)S(1)} %reshape_squeeze.6), channel_id=1, source_target_pairs={{0,1},{1,0},{2,3},{3,2},{128,131},{129,130},{130,129},{131,128},{2... | collective-permute-start | bytes 393224 | tf_op jit(solution)/shard_map/ppermute | solution.py:30
  56.1 30.0 %collective-permute-start.4 = (bf16[64,1024]{1,0:T(8,128)(2,1)S(1)}, bf16[64,1024]{1,0:T(8,128)(2,1)S(1)}, u32[]{:S(2)}, u32[]{:S(2)}) collective-permute-start(bf16[64,1024]{1,0:T(8,128)(2,1)S(1)} %reshape_squeeze.7), channel_id=1, source_target_pairs={{0,1},{1,0},{2,3},{3,2},{128,131},{129,130},{130,129},{131,128},{2... | collective-permute-start | bytes 393224 | tf_op jit(solution)/shard_map/ppermute | solution.py:30
  68.1 52.5 %collective-permute-start.1 = (bf16[128,1024]{1,0:T(8,128)(2,1)S(1)}, bf16[128,1024]{1,0:T(8,128)(2,1)S(1)}, u32[]{:S(2)}, u32[]{:S(2)}) collective-permute-start(bf16[128,1024]{1,0:T(8,128)(2,1)S(1)} %constant_dynamic-update-slice_fusion), channel_id=1, source_target_pairs={{0,3},{1,2},{2,1},{3,0},{128,129},{129,128},{130,131},{131,130},{2... | collective-permute-start | bytes 786440 | tf_op jit(solution)/shard_map/ppermute | solution.py:30
  86.1 48.6 %collective-permute-start.5 = (bf16[128,1024]{1,0:T(8,128)(2,1)S(1)}, bf16[128,1024]{1,0:T(8,128)(2,1)S(1)}, u32[]{:S(2)}, u32[]{:S(2)}) collective-permute-start(bf16[128,1024]{1,0:T(8,128)(2,1)S(1)} %constant_dynamic-update-slice_fusion.2), channel_id=1, source_target_pairs={{0,3},{1,2},{2,1},{3,0},{128,129},{129,128},{130,131},{131,130},{2... | collective-permute-start | bytes 786440 | tf_op jit(solution)/shard_map/ppermute | solution.py:30
  123.7 48.1 %collective-permute-start.2 = (bf16[128,1024]{1,0:T(8,128)(2,1)S(1)}, bf16[128,1024]{1,0:T(8,128)(2,1)S(1)}, u32[]{:S(2)}, u32[]{:S(2)}) collective-permute-start(bf16[128,1024]{1,0:T(8,128)(2,1)S(1)} %fusion.25), channel_id=1, source_target_pairs={{0,3},{1,2},{2,1},{3,0},{128,129},{129,128},{130,131},{131,130},{2... | collective-permute-start | bytes 786440 | tf_op jit(solution)/shard_map/ppermute | solution.py:30
  137.8 42.3 %collective-permute-start.6 = (bf16[128,1024]{1,0:T(8,128)(2,1)S(1)}, bf16[128,1024]{1,0:T(8,128)(2,1)S(1)}, u32[]{:S(2)}, u32[]{:S(2)}) collective-permute-start(bf16[128,1024]{1,0:T(8,128)(2,1)S(1)} %fusion.28), channel_id=1, source_target_pairs={{0,3},{1,2},{2,1},{3,0},{128,129},{129,128},{130,131},{131,130},{2... | collective-permute-start | bytes 786440 | tf_op jit(solution)/shard_map/ppermute | solution.py:30
  171.9 24.6 %collective-permute-start.3 = (bf16[64,1024]{1,0:T(8,128)(2,1)S(1)}, bf16[64,1024]{1,0:T(8,128)(2,1)S(1)}, u32[]{:S(2)}, u32[]{:S(2)}) collective-permute-start(bf16[64,1024]{1,0:T(8,128)(2,1)S(1)} %slice.117), channel_id=1, source_target_pairs={{0,1},{1,0},{2,3},{3,2},{128,131},{129,130},{130,129},{131,128},{2... | collective-permute-start | bytes 393224 | tf_op jit(solution)/shard_map/ppermute | solution.py:30
  180.2 17.7 %collective-permute-start.7 = (bf16[64,1024]{1,0:T(8,128)(2,1)S(1)}, bf16[64,1024]{1,0:T(8,128)(2,1)S(1)}, u32[]{:S(2)}, u32[]{:S(2)}) collective-permute-start(bf16[64,1024]{1,0:T(8,128)(2,1)S(1)} %slice.116), channel_id=1, source_target_pairs={{0,1},{1,0},{2,3},{3,2},{128,131},{129,130},{130,129},{131,128},{2... | collective-permute-start | bytes 393224 | tf_op jit(solution)/shard_map/ppermute | solution.py:30
where the time goes:
time: 239 us; the launch traced here: 238 us
  waiting for transfers between devices  78.2 us (33%)
  blocking collectives  73.4 us (31%)
  starting transfers between devices  66.6 us (28%)
  matrix products  16.4 us (7%)
  other arithmetic  2.87 us (1%)
    ppermute x8, waiting for transfers between devices, swap(): return lax.ppermute(value, ('dp', 'hid'), pairs)  78.2 us
    ppermute x8, starting transfers between devices, swap(): return lax.ppermute(value, ('dp', 'hid'), pairs)  66.6 us
    all_to_all x1, blocking collectives, layer(): lax.all_to_all(jnp.stack(results, axis=1), 'expert', 0, 0, tiled=True)  38.7 us
    all_to_all x1, blocking collectives, layer(): arrived = lax.all_to_all(grouped, 'expert', 0, 0, tiled=True)  34.7 us
    dot_general x4, matrix products, expert(): return jnp.dot(hidden, w_out, preferred_element_type=jnp.float32)  12.4 us
  transfers between devices with their start and end apart: 8, of which 5 were waited for; matrix products, arithmetic and copies ran while one was open for 5% of the time, Pallas kernels for 0%

commit v1 on v0

--- a/solution.py
+++ b/solution.py
@@ -4,6 +4,7 @@
 from jax.sharding import PartitionSpec as P
 
 SLOTS = 2
+RUN = 8
 
 
 def normal_rows(values):
@@ -28,6 +29,22 @@
         for i in range(ring)
     ]
     return lax.ppermute(value, ("dp", "hid"), pairs)
+
+
+def to_owners(value):
+    groups, owners, ring = (lax.axis_size(name) for name in ("dp", "expert", "hid"))
+    teams = [
+        [
+            (group * owners + owner) * ring
+            + (member + (group % 2 == 1 and owner % RUN < RUN // 2)) % ring
+            for owner in range(owners)
+        ]
+        for group in range(groups)
+        for member in range(ring)
+    ]
+    return lax.all_to_all(
+        value, ("dp", "expert", "hid"), 0, 0, axis_index_groups=teams, tiled=True
+    )
 
 
 def near(value):
@@ -73,12 +90,12 @@
     local_experts = w_in.shape[0]
     d_width = w_in.shape[1]
     grouped = slot_in.reshape(owners, local_experts, SLOTS, d_width)
-    arrived = lax.all_to_all(grouped, "expert", 0, 0, tiled=True)
+    arrived = to_owners(grouped)
     results = []
     for b in range(local_experts):
         own = arrived[:, b].reshape(-1, d_width)
         results.append(exchange(own, w_in[b], w_out[b]).reshape(owners, SLOTS, d_width))
-    results = lax.all_to_all(jnp.stack(results, axis=1), "expert", 0, 0, tiled=True)
+    results = to_owners(jnp.stack(results, axis=1))
     results = results.reshape(1, -1, d_width)
     return jnp.einsum("ite,ied->itd", combine, results, preferred_element_type=jnp.float32).astype(
         jnp.bfloat16

time: 239 us -> 247 us (1.033)
  the two profiles are of different devices: /device:TPU:24 before, /device:TPU:2 now
where the time goes in v1:
time: 247 us; the launch traced here: 246 us
  blocking collectives  88.4 us (36%)
  starting transfers between devices  86.7 us (35%)
  waiting for transfers between devices  51.2 us (21%)
  matrix products  16.4 us (7%)
  other arithmetic  2.87 us (1%)
    all_to_all x2, blocking collectives, to_owners(): lax.all_to_all(value, ('dp', 'expert', 'hid'), 0, 0, axis_index_groups=te...  88.4 us
    ppermute x8, starting transfers between devices, swap(): return lax.ppermute(value, ('dp', 'hid'), pairs)  86.7 us
    ppermute x8, waiting for transfers between devices, swap(): return lax.ppermute(value, ('dp', 'hid'), pairs)  51.2 us
    dot_general x4, matrix products, expert(): return jnp.dot(hidden, w_out, preferred_element_type=jnp.float32)  12.4 us
  transfers between devices with their start and end apart: 8, of which 4 were waited for; matrix products, arithmetic and copies ran while one was open for 5% of the time, Pallas kernels for 0%

profile of v1, /device:TPU:2, one launch (start us, length us, event | category | flops | bytes accessed | tf_op | source)
XLA Modules:
  0.0 246.4 jit_solution(16608913026527264959)
XLA Ops:
  0.0 1.2 fusion.32
  1.2 1.1 fusion.34
  2.3 1.6 fusion.134
  3.9 1.3 convolution_convert_fusion.1
  5.3 31.9 %all_to_all.10 = bf16[32,2,2,1024]{3,2,1,0:T(2,128)(2,1)S(1)} all-to-all(bf16[32,2,2,1024]{3,2,1,0:T(2,128)(2,1)S(1)} %reshape.61), channel_id=1, replica_groups={{0,4,8,12,16,20,24,28,32,36,40,44,48,52,56,60,64,68,72,76,80,84,88,92,9..., dimensions={0} | all-to-all | bytes 524288 | tf_op jit(solution)/shard_map/all_to_all | solution.py:45
  37.4 14.1 %collective-permute-start = (bf16[64,1024]{1,0:T(8,128)(2,1)S(1)}, bf16[64,1024]{1,0:T(8,128)(2,1)S(1)}, u32[]{:S(2)}, u32[]{:S(2)}) collective-permute-start(bf16[64,1024]{1,0:T(8,128)(2,1)S(1)} %reshape_squeeze.6), channel_id=1, source_target_pairs={{0,1},{1,0},{2,3},{3,2},{128,131},{129,130},{130,129},{131,128},{2... | collective-permute-start | bytes 393224 | tf_op jit(solution)/shard_map/ppermute | solution.py:31
  51.6 1.9 collective-permute-start.4
  53.6 9.1 %collective-permute-done = bf16[64,1024]{1,0:T(8,128)(2,1)S(1)} collective-permute-done((bf16[64,1024]{1,0:T(8,128)(2,1)S(1)}, bf16[64,1024]{1,0:T(8,128)(2,1)S(1)}, u32[]{:S(2)}, u32[]{:S(2)}) %collective-permute-start) | collective-permute-done | bytes 131104 | tf_op jit(solution)/shard_map/ppermute | solution.py:31
  62.7 5.7 %collective-permute-start.1 = (bf16[128,1024]{1,0:T(8,128)(2,1)S(1)}, bf16[128,1024]{1,0:T(8,128)(2,1)S(1)}, u32[]{:S(2)}, u32[]{:S(2)}) collective-permute-start(bf16[128,1024]{1,0:T(8,128)(2,1)S(1)} %constant_dynamic-update-slice_fusion), channel_id=1, source_target_pairs={{0,3},{1,2},{2,1},{3,0},{128,129},{129,128},{130,131},{131,130},{2... | collective-permute-start | bytes 786440 | tf_op jit(solution)/shard_map/ppermute | solution.py:31
  68.4 6.8 %collective-permute-done.4 = bf16[64,1024]{1,0:T(8,128)(2,1)S(1)} collective-permute-done((bf16[64,1024]{1,0:T(8,128)(2,1)S(1)}, bf16[64,1024]{1,0:T(8,128)(2,1)S(1)}, u32[]{:S(2)}, u32[]{:S(2)}) %collective-permute-start.4) | collective-permute-done | bytes 131104 | tf_op jit(solution)/shard_map/ppermute | solution.py:31
  75.2 18.0 %collective-permute-start.5 = (bf16[128,1024]{1,0:T(8,128)(2,1)S(1)}, bf16[128,1024]{1,0:T(8,128)(2,1)S(1)}, u32[]{:S(2)}, u32[]{:S(2)}) collective-permute-start(bf16[128,1024]{1,0:T(8,128)(2,1)S(1)} %constant_dynamic-update-slice_fusion.2), channel_id=1, source_target_pairs={{0,3},{1,2},{2,1},{3,0},{128,129},{129,128},{130,131},{131,130},{2... | collective-permute-start | bytes 786440 | tf_op jit(solution)/shard_map/ppermute | solution.py:31
  93.2 3.1 %fusion.10 = f32[128,1024]{1,0:T(8,128)S(1)} fusion(bf16[2,1024,1024]{2,1,0:T(8,128)(2,1)} %param.7, bf16[128,1024]{1,0:T(8,128)(2,1)S(1)} %constant_dynamic-update-slice_fusion, bf16[2,1024,1024]{2,1,0:T(8,128)(2,1)} %param.6), kind=kOutput, calls=%fused_computation.10 | convolution fusion | flops 538050560 | bytes 4980736 | tf_op jit(solution)/shard_map/dot_general | solution.py:62
  96.3 3.1 %fusion.2 = f32[128,1024]{1,0:T(8,128)S(1)} fusion(bf16[2,1024,1024]{2,1,0:T(8,128)(2,1)} %param.7, bf16[128,1024]{1,0:T(8,128)(2,1)S(1)} %constant_dynamic-update-slice_fusion.2, bf16[2,1024,1024]{2,1,0:T(8,128)(2,1)} %param.6), kind=kOutput, calls=%fused_computation.2 | convolution fusion | flops 538050560 | bytes 4980736 | tf_op jit(solution)/shard_map/dot_general | solution.py:62
  99.4 3.1 %fusion.25 = bf16[128,1024]{1,0:T(8,128)(2,1)S(1)} fusion(bf16[2,1024,1024]{2,1,0:T(8,128)(2,1)} %param.7, bf16[128,1024]{1,0:T(8,128)(2,1)S(1)} %collective-permute-done.1, bf16[2,1024,1024]{2,1,0:T(8,128)(2,1)} %param.6), kind=kOutput, calls=%fused_computation.28 | convolution fusion | flops 538181632 | bytes 4718592 | tf_op jit(solution)/shard_map/dot_general | solution.py:62
  102.5 1.9 collective-permute-start.2
  104.4 3.1 %fusion.28 = bf16[128,1024]{1,0:T(8,128)(2,1)S(1)} fusion(bf16[2,1024,1024]{2,1,0:T(8,128)(2,1)} %param.7, bf16[128,1024]{1,0:T(8,128)(2,1)S(1)} %collective-permute-done.5, bf16[2,1024,1024]{2,1,0:T(8,128)(2,1)} %param.6), kind=kOutput, calls=%fused_computation.29 | convolution fusion | flops 538181632 | bytes 4718592 | tf_op jit(solution)/shard_map/dot_general | solution.py:62
  107.5 13.1 %collective-permute-start.6 = (bf16[128,1024]{1,0:T(8,128)(2,1)S(1)}, bf16[128,1024]{1,0:T(8,128)(2,1)S(1)}, u32[]{:S(2)}, u32[]{:S(2)}) collective-permute-start(bf16[128,1024]{1,0:T(8,128)(2,1)S(1)} %fusion.28), channel_id=1, source_target_pairs={{0,3},{1,2},{2,1},{3,0},{128,129},{129,128},{130,131},{131,130},{2... | collective-permute-start | bytes 786440 | tf_op jit(solution)/shard_map/ppermute | solution.py:31
  120.6 32.0 %collective-permute-done.2 = bf16[128,1024]{1,0:T(8,128)(2,1)S(1)} collective-permute-done((bf16[128,1024]{1,0:T(8,128)(2,1)S(1)}, bf16[128,1024]{1,0:T(8,128)(2,1)S(1)}, u32[]{:S(2)}, u32[]{:S(2)}) %collective-permute-start.2) | collective-permute-done | bytes 262176 | tf_op jit(solution)/shard_map/ppermute | solution.py:31
  152.8 4.5 %collective-permute-start.3 = (bf16[64,1024]{1,0:T(8,128)(2,1)S(1)}, bf16[64,1024]{1,0:T(8,128)(2,1)S(1)}, u32[]{:S(2)}, u32[]{:S(2)}) collective-permute-start(bf16[64,1024]{1,0:T(8,128)(2,1)S(1)} %slice.117), channel_id=1, source_target_pairs={{0,1},{1,0},{2,3},{3,2},{128,131},{129,130},{130,129},{131,128},{2... | collective-permute-start | bytes 393224 | tf_op jit(solution)/shard_map/ppermute | solution.py:31
  157.3 27.5 %collective-permute-start.7 = (bf16[64,1024]{1,0:T(8,128)(2,1)S(1)}, bf16[64,1024]{1,0:T(8,128)(2,1)S(1)}, u32[]{:S(2)}, u32[]{:S(2)}) collective-permute-start(bf16[64,1024]{1,0:T(8,128)(2,1)S(1)} %slice.116), channel_id=1, source_target_pairs={{0,1},{1,0},{2,3},{3,2},{128,131},{129,130},{130,129},{131,128},{2... | collective-permute-start | bytes 393224 | tf_op jit(solution)/shard_map/ppermute | solution.py:31
  185.0 3.2 %collective-permute-done.7 = bf16[64,1024]{1,0:T(8,128)(2,1)S(1)} collective-permute-done((bf16[64,1024]{1,0:T(8,128)(2,1)S(1)}, bf16[64,1024]{1,0:T(8,128)(2,1)S(1)}, u32[]{:S(2)}, u32[]{:S(2)}) %collective-permute-start.7) | collective-permute-done | bytes 131104 | tf_op jit(solution)/shard_map/ppermute | solution.py:31
  188.3 0.3 pad_maximum_fusion
  188.6 56.6 %all_to_all.11 = bf16[32,2,2,1024]{3,2,1,0:T(2,128)(2,1)S(1)} all-to-all(bf16[32,2,2,1024]{3,2,1,0:T(2,128)(2,1)S(1)} %pad_maximum_fusion), channel_id=1, replica_groups={{0,4,8,12,16,20,24,28,32,36,40,44,48,52,56,60,64,68,72,76,80,84,88,92,9..., dimensions={0} | all-to-all | bytes 524288 | tf_op jit(solution)/shard_map/all_to_all | solution.py:45
  245.3 1.1 fusion.24
  (23 shorter events, 0.9 us)
Async XLA Ops:
  37.4 25.2 %collective-permute-start = (bf16[64,1024]{1,0:T(8,128)(2,1)S(1)}, bf16[64,1024]{1,0:T(8,128)(2,1)S(1)}, u32[]{:S(2)}, u32[]{:S(2)}) collective-permute-start(bf16[64,1024]{1,0:T(8,128)(2,1)S(1)} %reshape_squeeze.6), channel_id=1, source_target_pairs={{0,1},{1,0},{2,3},{3,2},{128,131},{129,130},{130,129},{131,128},{2... | collective-permute-start | bytes 393224 | tf_op jit(solution)/shard_map/ppermute | solution.py:31
  51.6 23.6 %collective-permute-start.4 = (bf16[64,1024]{1,0:T(8,128)(2,1)S(1)}, bf16[64,1024]{1,0:T(8,128)(2,1)S(1)}, u32[]{:S(2)}, u32[]{:S(2)}) collective-permute-start(bf16[64,1024]{1,0:T(8,128)(2,1)S(1)} %reshape_squeeze.7), channel_id=1, source_target_pairs={{0,1},{1,0},{2,3},{3,2},{128,131},{129,130},{130,129},{131,128},{2... | collective-permute-start | bytes 393224 | tf_op jit(solution)/shard_map/ppermute | solution.py:31
  62.7 36.7 %collective-permute-start.1 = (bf16[128,1024]{1,0:T(8,128)(2,1)S(1)}, bf16[128,1024]{1,0:T(8,128)(2,1)S(1)}, u32[]{:S(2)}, u32[]{:S(2)}) collective-permute-start(bf16[128,1024]{1,0:T(8,128)(2,1)S(1)} %constant_dynamic-update-slice_fusion), channel_id=1, source_target_pairs={{0,3},{1,2},{2,1},{3,0},{128,129},{129,128},{130,131},{131,130},{2... | collective-permute-start | bytes 786440 | tf_op jit(solution)/shard_map/ppermute | solution.py:31
  75.2 29.2 %collective-permute-start.5 = (bf16[128,1024]{1,0:T(8,128)(2,1)S(1)}, bf16[128,1024]{1,0:T(8,128)(2,1)S(1)}, u32[]{:S(2)}, u32[]{:S(2)}) collective-permute-start(bf16[128,1024]{1,0:T(8,128)(2,1)S(1)} %constant_dynamic-update-slice_fusion.2), channel_id=1, source_target_pairs={{0,3},{1,2},{2,1},{3,0},{128,129},{129,128},{130,131},{131,130},{2... | collective-permute-start | bytes 786440 | tf_op jit(solution)/shard_map/ppermute | solution.py:31
  102.5 50.2 %collective-permute-start.2 = (bf16[128,1024]{1,0:T(8,128)(2,1)S(1)}, bf16[128,1024]{1,0:T(8,128)(2,1)S(1)}, u32[]{:S(2)}, u32[]{:S(2)}) collective-permute-start(bf16[128,1024]{1,0:T(8,128)(2,1)S(1)} %fusion.25), channel_id=1, source_target_pairs={{0,3},{1,2},{2,1},{3,0},{128,129},{129,128},{130,131},{131,130},{2... | collective-permute-start | bytes 786440 | tf_op jit(solution)/shard_map/ppermute | solution.py:31
  107.5 49.7 %collective-permute-start.6 = (bf16[128,1024]{1,0:T(8,128)(2,1)S(1)}, bf16[128,1024]{1,0:T(8,128)(2,1)S(1)}, u32[]{:S(2)}, u32[]{:S(2)}) collective-permute-start(bf16[128,1024]{1,0:T(8,128)(2,1)S(1)} %fusion.28), channel_id=1, source_target_pairs={{0,3},{1,2},{2,1},{3,0},{128,129},{129,128},{130,131},{131,130},{2... | collective-permute-start | bytes 786440 | tf_op jit(solution)/shard_map/ppermute | solution.py:31
  152.8 32.1 %collective-permute-start.3 = (bf16[64,1024]{1,0:T(8,128)(2,1)S(1)}, bf16[64,1024]{1,0:T(8,128)(2,1)S(1)}, u32[]{:S(2)}, u32[]{:S(2)}) collective-permute-start(bf16[64,1024]{1,0:T(8,128)(2,1)S(1)} %slice.117), channel_id=1, source_target_pairs={{0,1},{1,0},{2,3},{3,2},{128,131},{129,130},{130,129},{131,128},{2... | collective-permute-start | bytes 393224 | tf_op jit(solution)/shard_map/ppermute | solution.py:31
  157.3 30.8 %collective-permute-start.7 = (bf16[64,1024]{1,0:T(8,128)(2,1)S(1)}, bf16[64,1024]{1,0:T(8,128)(2,1)S(1)}, u32[]{:S(2)}, u32[]{:S(2)}) collective-permute-start(bf16[64,1024]{1,0:T(8,128)(2,1)S(1)} %slice.116), channel_id=1, source_target_pairs={{0,1},{1,0},{2,3},{3,2},{128,131},{129,130},{130,129},{131,128},{2... | collective-permute-start | bytes 393224 | tf_op jit(solution)/shard_map/ppermute | solution.py:31

commit v2 on v1

v2 whole, which is shorter than its diff:
```python
import jax
import jax.numpy as jnp
from jax import lax
from jax.experimental import pallas as pl
from jax.experimental.pallas import tpu as pltpu
from jax.sharding import PartitionSpec as P

SLOTS = 2
RUN = 8


def route(images_ref, keys_ref, slots_ref, combine_ref):
    keys = keys_ref[...].astype(jnp.float32)
    unit_keys = (keys * lax.rsqrt(jnp.sum(keys * keys, axis=0, keepdims=True) + 1e-06)).astype(
        jnp.bfloat16
    )
    tokens = images_ref[...]
    floats = tokens.astype(jnp.float32)
    normed = (floats * lax.rsqrt(jnp.mean(floats * floats, axis=1, keepdims=True) + 1e-06)).astype(
        jnp.bfloat16
    )
    powers = jnp.exp(2.0 * jnp.dot(normed, unit_keys, preferred_element_type=jnp.float32))
    dispatch = (powers / jnp.sum(powers, axis=0, keepdims=True)).astype(jnp.bfloat16)
    combine_ref[...] = (powers / jnp.sum(powers, axis=1, keepdims=True)).astype(jnp.bfloat16)
    slots_ref[...] = lax.dot_general(
        dispatch, tokens, (((0,), (0,)), ((), ())), preferred_element_type=jnp.float32
    ).astype(jnp.bfloat16)


def router(tokens, slot_keys):
    (rows, width), columns = tokens.shape, slot_keys.shape[1]
    return pl.pallas_call(
        route,
        out_shape=(
            jax.ShapeDtypeStruct((columns, width), jnp.bfloat16),
            jax.ShapeDtypeStruct((rows, columns), jnp.bfloat16),
        ),
        compiler_params=pltpu.CompilerParams(vmem_limit_bytes=60 << 20),
    )(tokens, slot_keys)


def onward(value):
    groups, ring = lax.axis_size("dp"), lax.axis_size("hid")
    pairs = []
    for group in range(groups):
        step = 1 if group % 2 == 0 else ring - 1
        pairs += [(group * ring + i, group * ring + (i + step) % ring) for i in range(ring)]
    return lax.ppermute(value, ("dp", "hid"), pairs)


def to_owners(value):
    groups, owners, ring = (lax.axis_size(name) for name in ("dp", "expert", "hid"))
    teams = [
        [
            (group * owners + owner) * ring
            + (member + (group % 2 == 1 and owner % RUN < RUN // 2)) % ring
            for owner in range(owners)
        ]
        for group in range(groups)
        for member in range(ring)
    ]
    return lax.all_to_all(
        value, ("dp", "expert", "hid"), 0, 0, axis_index_groups=teams, tiled=True
    )


def expert(rows, w_in, w_out):
    hidden = jax.nn.gelu(
        jnp.dot(rows, w_in, preferred_element_type=jnp.float32), approximate=True
    ).astype(jnp.bfloat16)
    return jnp.dot(hidden, w_out, preferred_element_type=jnp.float32)


def rings(owns, w_in, w_out):
    count, stops, chunks = owns[0].shape[0], lax.axis_size("hid"), range(len(owns))
    blocks = [onward(owns[c]) for c in chunks]
    totals = [expert(blocks[c], w_in[c], w_out[c]).astype(jnp.bfloat16) for c in chunks]
    for step in range(2, stops):
        for c in chunks:
            both = onward(jnp.concatenate([blocks[c], totals[c]]))
            if step == stops - 1 and c > 0:
                both, _ = lax.optimization_barrier((both, totals[c - 1]))
            blocks[c], total = both[:count], both[count:].astype(jnp.float32)
            if step < stops - 1:
                totals[c] = (expert(blocks[c], w_in[c], w_out[c]) + total).astype(jnp.bfloat16)
            else:
                last = expert(jnp.concatenate([blocks[c], owns[c]]), w_in[c], w_out[c])
                totals[c] = (last[:count] + total).astype(jnp.bfloat16)
                blocks[c] = last[count:]
    totals = [onward(totals[c]).astype(jnp.float32) for c in chunks]
    return [(blocks[c] + totals[c]).astype(jnp.bfloat16) for c in chunks]


def layer(images_in, slot_keys, w_in, w_out):
    slot_in, combine = router(images_in[0], slot_keys)
    owners = lax.axis_size("expert")
    local_experts = w_in.shape[0]
    d_width = w_in.shape[1]
    grouped = slot_in.reshape(owners, local_experts, SLOTS, d_width)
    arrived = to_owners(grouped)
    owns = [arrived[:, b].reshape(-1, d_width) for b in range(local_experts)]
    results = [total.reshape(owners, SLOTS, d_width) for total in rings(owns, w_in, w_out)]
    results = to_owners(jnp.stack(results, axis=1))
    results = results.reshape(-1, d_width)
    mixed = jnp.dot(combine, results, preferred_element_type=jnp.float32)
    return mixed.astype(jnp.bfloat16)[None]


def solution(mesh):
    return jax.shard_map(
        layer,
        mesh=mesh,
        in_specs=(
            P(("dp", "expert", "hid"), None, None),
            P(),
            P("expert", None, "hid"),
            P("expert", "hid", None),
        ),
        out_specs=P(("dp", "expert", "hid"), None, None),
        check_vma=False,
    )
```

time: 247 us -> 229 us (0.927)
  the two profiles are of different devices: /device:TPU:2 before, /device:TPU:8 now
where the time goes in v2:
time: 229 us; the launch traced here: 228 us
  waiting for transfers between devices  78.5 us (34%)
  starting transfers between devices  73.5 us (32%)
  blocking collectives  51.4 us (22%)
  matrix products  19.7 us (9%)
  Pallas kernels  2.63 us (1%)
    ppermute x8, waiting for transfers between devices, onward(): return lax.ppermute(value, ('dp', 'hid'), pairs)  78.5 us
    ppermute x8, starting transfers between devices, onward(): return lax.ppermute(value, ('dp', 'hid'), pairs)  73.5 us
    all_to_all x2, blocking collectives, to_owners(): lax.all_to_all(value, ('dp', 'expert', 'hid'), 0, 0, axis_index_groups=te...  51.4 us
    dot_general x6, matrix products, expert(): return jnp.dot(hidden, w_out, preferred_element_type=jnp.float32)  18.7 us
  transfers between devices with their start and end apart: 8, of which 5 were waited for; matrix products, arithmetic and copies ran while one was open for 8% of the time, Pallas kernels for 0%

profile of v2, /device:TPU:8, one launch (start us, length us, event | category | flops | bytes accessed | tf_op | source)
XLA Modules:
  0.0 228.1 jit_solution(13122380247823703488)
XLA Ops:
  0.0 2.6 %shard_map.46 = (bf16[128,1024]{1,0:T(8,128)(2,1)}, bf16[256,128]{1,0:T(8,128)(2,1)}) custom-call(bf16[256,1024]{1,0:T(8,128)(2,1)} %bitcast.93, bf16[1024,128]{1,0:T(8,128)(2,1)} %keys_ref.1), custom_call_target="tpu_custom_call" | custom-call | tf_op jit(solution)/shard_map/pallas_call | solution.py:32
  2.6 1.0 reshape.6
  3.7 32.7 %all_to_all.10 = bf16[32,2,2,1024]{3,2,1,0:T(2,128)(2,1)S(1)} all-to-all(bf16[32,2,2,1024]{3,2,1,0:T(2,128)(2,1)S(1)} %reshape.6), channel_id=1, replica_groups={{0,4,8,12,16,20,24,28,32,36,40,44,48,52,56,60,64,68,72,76,80,84,88,92,9..., dimensions={0} | all-to-all | bytes 524288 | tf_op jit(solution)/shard_map/all_to_all | solution.py:62
  36.6 14.8 %collective-permute-start = (bf16[64,1024]{1,0:T(8,128)(2,1)S(1)}, bf16[64,1024]{1,0:T(8,128)(2,1)S(1)}, u32[]{:S(2)}, u32[]{:S(2)}) collective-permute-start(bf16[64,1024]{1,0:T(8,128)(2,1)S(1)} %reshape_squeeze.6), channel_id=1, source_target_pairs={{0,1},{1,2},{2,3},{3,0},{128,131},{129,128},{130,129},{131,130},{2... | collective-permute-start | bytes 393224 | tf_op jit(solution)/shard_map/ppermute | solution.py:48
  51.5 7.6 %collective-permute-start.4 = (bf16[64,1024]{1,0:T(8,128)(2,1)S(1)}, bf16[64,1024]{1,0:T(8,128)(2,1)S(1)}, u32[]{:S(2)}, u32[]{:S(2)}) collective-permute-start(bf16[64,1024]{1,0:T(8,128)(2,1)S(1)} %reshape_squeeze.7), channel_id=1, source_target_pairs={{0,1},{1,2},{2,3},{3,0},{128,131},{129,128},{130,129},{131,130},{2... | collective-permute-start | bytes 393224 | tf_op jit(solution)/shard_map/ppermute | solution.py:48
  59.1 3.1 %fusion.37 = bf16[64,1024]{1,0:T(8,128)(2,1)S(1)} fusion(bf16[2,1024,1024]{2,1,0:T(8,128)(2,1)} %param.7, bf16[64,1024]{1,0:T(8,128)(2,1)S(1)} %collective-permute-done, bf16[2,1024,1024]{2,1,0:T(8,128)(2,1)} %param.6), kind=kOutput, calls=%fused_computation.38 | convolution fusion | flops 269090816 | bytes 4456448 | tf_op jit(solution)/shard_map/dot_general | solution.py:71
  62.2 11.7 %collective-permute-start.1 = (bf16[128,1024]{1,0:T(8,128)(2,1)S(1)}, bf16[128,1024]{1,0:T(8,128)(2,1)S(1)}, u32[]{:S(2)}, u32[]{:S(2)}) collective-permute-start(bf16[128,1024]{1,0:T(8,128)(2,1)S(1)} %pad_maximum_fusion), channel_id=1, source_target_pairs={{0,1},{1,2},{2,3},{3,0},{128,131},{129,128},{130,129},{131,130},{2... | collective-permute-start | bytes 786440 | tf_op jit(solution)/shard_map/ppermute | solution.py:48
  73.9 2.2 collective-permute-done.4
  76.1 3.1 %fusion.40 = bf16[64,1024]{1,0:T(8,128)(2,1)S(1)} fusion(bf16[2,1024,1024]{2,1,0:T(8,128)(2,1)} %param.7, bf16[64,1024]{1,0:T(8,128)(2,1)S(1)} %collective-permute-done.4, bf16[2,1024,1024]{2,1,0:T(8,128)(2,1)} %param.6), kind=kOutput, calls=%fused_computation.39 | convolution fusion | flops 269090816 | bytes 4456448 | tf_op jit(solution)/shard_map/dot_general | solution.py:71
  79.2 9.9 %collective-permute-start.5 = (bf16[128,1024]{1,0:T(8,128)(2,1)S(1)}, bf16[128,1024]{1,0:T(8,128)(2,1)S(1)}, u32[]{:S(2)}, u32[]{:S(2)}) collective-permute-start(bf16[128,1024]{1,0:T(8,128)(2,1)S(1)} %pad_maximum_fusion.2), channel_id=1, source_target_pairs={{0,1},{1,2},{2,3},{3,0},{128,131},{129,128},{130,129},{131,130},{2... | collective-permute-start | bytes 786440 | tf_op jit(solution)/shard_map/ppermute | solution.py:48
  89.2 38.5 %collective-permute-done.1 = bf16[128,1024]{1,0:T(8,128)(2,1)S(1)} collective-permute-done((bf16[128,1024]{1,0:T(8,128)(2,1)S(1)}, bf16[128,1024]{1,0:T(8,128)(2,1)S(1)}, u32[]{:S(2)}, u32[]{:S(2)}) %collective-permute-start.1) | collective-permute-done | bytes 262176 | tf_op jit(solution)/shard_map/ppermute | solution.py:48
  127.6 3.1 %fusion.104 = bf16[64,1024]{1,0:T(8,128)(2,1)S(1)} fusion(bf16[2,1024,1024]{2,1,0:T(8,128)(2,1)} %param.7, bf16[2,1024,1024]{2,1,0:T(8,128)(2,1)} %param.6, bf16[128,1024]{1,0:T(8,128)(2,1)S(1)} %collective-permute-done.1), kind=kOutput, calls=%fused_computation.79 | convolution fusion | flops 269221888 | bytes 4587520 | tf_op jit(solution)/shard_map/dot_general | solution.py:71
  130.8 9.9 %collective-permute-start.2 = (bf16[128,1024]{1,0:T(8,128)(2,1)S(1)}, bf16[128,1024]{1,0:T(8,128)(2,1)S(1)}, u32[]{:S(2)}, u32[]{:S(2)}) collective-permute-start(bf16[128,1024]{1,0:T(8,128)(2,1)S(1)} %pad_maximum_fusion.1), channel_id=1, source_target_pairs={{0,1},{1,2},{2,3},{3,0},{128,131},{129,128},{130,129},{131,130},{2... | collective-permute-start | bytes 786440 | tf_op jit(solution)/shard_map/ppermute | solution.py:48
  140.6 3.1 %fusion.142 = bf16[64,1024]{1,0:T(8,128)(2,1)S(1)} fusion(bf16[2,1024,1024]{2,1,0:T(8,128)(2,1)} %param.7, bf16[2,1024,1024]{2,1,0:T(8,128)(2,1)} %param.6, bf16[128,1024]{1,0:T(8,128)(2,1)S(1)} %collective-permute-done.5), kind=kOutput, calls=%fused_computation.97 | convolution fusion | flops 269221888 | bytes 4587520 | tf_op jit(solution)/shard_map/dot_general | solution.py:71
  143.8 6.0 %collective-permute-start.6 = (bf16[128,1024]{1,0:T(8,128)(2,1)S(1)}, bf16[128,1024]{1,0:T(8,128)(2,1)S(1)}, u32[]{:S(2)}, u32[]{:S(2)}) collective-permute-start(bf16[128,1024]{1,0:T(8,128)(2,1)S(1)} %pad_maximum_fusion.3), channel_id=1, source_target_pairs={{0,1},{1,2},{2,3},{3,0},{128,131},{129,128},{130,129},{131,130},{2... | collective-permute-start | bytes 786440 | tf_op jit(solution)/shard_map/ppermute | solution.py:48
  149.8 29.7 %collective-permute-done.2 = bf16[128,1024]{1,0:T(8,128)(2,1)S(1)} collective-permute-done((bf16[128,1024]{1,0:T(8,128)(2,1)S(1)}, bf16[128,1024]{1,0:T(8,128)(2,1)S(1)}, u32[]{:S(2)}, u32[]{:S(2)}) %collective-permute-start.2) | collective-permute-done | bytes 262176 | tf_op jit(solution)/shard_map/ppermute | solution.py:48
  179.5 3.1 %fusion.12 = f32[128,1024]{1,0:T(8,128)S(1)} fusion(bf16[2,1024,1024]{2,1,0:T(8,128)(2,1)} %param.7, bf16[2,1024,1024]{2,1,0:T(8,128)(2,1)} %param.6, bf16[64,1024]{1,0:T(8,128)(2,1)S(1)} %reshape_squeeze.6, bf16[64,1024]{1,0:T(8,128)(2,1)S(1)} %slice.83), kind=kOutput, calls=%fused_computation.12 | convolution fusion | flops 538574848 | bytes 4980736 | tf_op jit(solution)/shard_map/dot_general | solution.py:71
  182.6 6.4 %collective-permute-start.3 = (bf16[64,1024]{1,0:T(8,128)(2,1)S(1)}, bf16[64,1024]{1,0:T(8,128)(2,1)S(1)}, u32[]{:S(2)}, u32[]{:S(2)}) collective-permute-start(bf16[64,1024]{1,0:T(8,128)(2,1)S(1)} %fusion.149), channel_id=1, source_target_pairs={{0,1},{1,2},{2,3},{3,0},{128,131},{129,128},{130,129},{131,130},{2... | collective-permute-start | bytes 393224 | tf_op jit(solution)/shard_map/ppermute | solution.py:48
  189.0 3.1 %fusion = f32[128,1024]{1,0:T(8,128)S(1)} fusion(bf16[2,1024,1024]{2,1,0:T(8,128)(2,1)} %param.7, bf16[2,1024,1024]{2,1,0:T(8,128)(2,1)} %param.6, bf16[64,1024]{1,0:T(8,128)(2,1)S(1)} %reshape_squeeze.7, bf16[64,1024]{1,0:T(8,128)(2,1)S(1)} %slice.76), kind=kOutput, calls=%fused_computation | convolution fusion | flops 538574848 | bytes 4980736 | tf_op jit(solution)/shard_map/dot_general | solution.py:71
  192.2 7.3 %collective-permute-start.7 = (bf16[64,1024]{1,0:T(8,128)(2,1)S(1)}, bf16[64,1024]{1,0:T(8,128)(2,1)S(1)}, u32[]{:S(2)}, u32[]{:S(2)}) collective-permute-start(bf16[64,1024]{1,0:T(8,128)(2,1)S(1)} %fusion.147), channel_id=1, source_target_pairs={{0,1},{1,2},{2,3},{3,0},{128,131},{129,128},{130,129},{131,130},{2... | collective-permute-start | bytes 393224 | tf_op jit(solution)/shard_map/ppermute | solution.py:48
  199.7 8.1 %collective-permute-done.7 = bf16[64,1024]{1,0:T(8,128)(2,1)S(1)} collective-permute-done((bf16[64,1024]{1,0:T(8,128)(2,1)S(1)}, bf16[64,1024]{1,0:T(8,128)(2,1)S(1)}, u32[]{:S(2)}, u32[]{:S(2)}) %collective-permute-start.7) | collective-permute-done | bytes 131104 | tf_op jit(solution)/shard_map/ppermute | solution.py:48
  207.9 0.3 pad_maximum_fusion.4
  208.2 18.7 %all_to_all.11 = bf16[32,2,2,1024]{3,2,1,0:T(2,128)(2,1)S(1)} all-to-all(bf16[32,2,2,1024]{3,2,1,0:T(2,128)(2,1)S(1)} %pad_maximum_fusion.4), channel_id=1, replica_groups={{0,4,8,12,16,20,24,28,32,36,40,44,48,52,56,60,64,68,72,76,80,84,88,92,9..., dimensions={0} | all-to-all | bytes 524288 | tf_op jit(solution)/shard_map/all_to_all | solution.py:62
  227.0 1.1 fusion.36
  (24 shorter events, 0.8 us)
Async XLA Ops:
  36.6 22.4 %collective-permute-start = (bf16[64,1024]{1,0:T(8,128)(2,1)S(1)}, bf16[64,1024]{1,0:T(8,128)(2,1)S(1)}, u32[]{:S(2)}, u32[]{:S(2)}) collective-permute-start(bf16[64,1024]{1,0:T(8,128)(2,1)S(1)} %reshape_squeeze.6), channel_id=1, source_target_pairs={{0,1},{1,2},{2,3},{3,0},{128,131},{129,128},{130,129},{131,130},{2... | collective-permute-start | bytes 393224 | tf_op jit(solution)/shard_map/ppermute | solution.py:48
  51.5 24.6 %collective-permute-start.4 = (bf16[64,1024]{1,0:T(8,128)(2,1)S(1)}, bf16[64,1024]{1,0:T(8,128)(2,1)S(1)}, u32[]{:S(2)}, u32[]{:S(2)}) collective-permute-start(bf16[64,1024]{1,0:T(8,128)(2,1)S(1)} %reshape_squeeze.7), channel_id=1, source_target_pairs={{0,1},{1,2},{2,3},{3,0},{128,131},{129,128},{130,129},{131,130},{2... | collective-permute-start | bytes 393224 | tf_op jit(solution)/shard_map/ppermute | solution.py:48
  62.2 65.4 %collective-permute-start.1 = (bf16[128,1024]{1,0:T(8,128)(2,1)S(1)}, bf16[128,1024]{1,0:T(8,128)(2,1)S(1)}, u32[]{:S(2)}, u32[]{:S(2)}) collective-permute-start(bf16[128,1024]{1,0:T(8,128)(2,1)S(1)} %pad_maximum_fusion), channel_id=1, source_target_pairs={{0,1},{1,2},{2,3},{3,0},{128,131},{129,128},{130,129},{131,130},{2... | collective-permute-start | bytes 786440 | tf_op jit(solution)/shard_map/ppermute | solution.py:48
  79.2 61.4 %collective-permute-start.5 = (bf16[128,1024]{1,0:T(8,128)(2,1)S(1)}, bf16[128,1024]{1,0:T(8,128)(2,1)S(1)}, u32[]{:S(2)}, u32[]{:S(2)}) collective-permute-start(bf16[128,1024]{1,0:T(8,128)(2,1)S(1)} %pad_maximum_fusion.2), channel_id=1, source_target_pairs={{0,1},{1,2},{2,3},{3,0},{128,131},{129,128},{130,129},{131,130},{2... | collective-permute-start | bytes 786440 | tf_op jit(solution)/shard_map/ppermute | solution.py:48
  130.8 48.7 %collective-permute-start.2 = (bf16[128,1024]{1,0:T(8,128)(2,1)S(1)}, bf16[128,1024]{1,0:T(8,128)(2,1)S(1)}, u32[]{:S(2)}, u32[]{:S(2)}) collective-permute-start(bf16[128,1024]{1,0:T(8,128)(2,1)S(1)} %pad_maximum_fusion.1), channel_id=1, source_target_pairs={{0,1},{1,2},{2,3},{3,0},{128,131},{129,128},{130,129},{131,130},{2... | collective-permute-start | bytes 786440 | tf_op jit(solution)/shard_map/ppermute | solution.py:48
  143.8 45.2 %collective-permute-start.6 = (bf16[128,1024]{1,0:T(8,128)(2,1)S(1)}, bf16[128,1024]{1,0:T(8,128)(2,1)S(1)}, u32[]{:S(2)}, u32[]{:S(2)}) collective-permute-start(bf16[128,1024]{1,0:T(8,128)(2,1)S(1)} %pad_maximum_fusion.3), channel_id=1, source_target_pairs={{0,1},{1,2},{2,3},{3,0},{128,131},{129,128},{130,129},{131,130},{2... | collective-permute-start | bytes 786440 | tf_op jit(solution)/shard_map/ppermute | solution.py:48
  182.6 17.0 %collective-permute-start.3 = (bf16[64,1024]{1,0:T(8,128)(2,1)S(1)}, bf16[64,1024]{1,0:T(8,128)(2,1)S(1)}, u32[]{:S(2)}, u32[]{:S(2)}) collective-permute-start(bf16[64,1024]{1,0:T(8,128)(2,1)S(1)} %fusion.149), channel_id=1, source_target_pairs={{0,1},{1,2},{2,3},{3,0},{128,131},{129,128},{130,129},{131,130},{2... | collective-permute-start | bytes 393224 | tf_op jit(solution)/shard_map/ppermute | solution.py:48
  189.0 37.9 %copy-start = (bf16[256,128]{1,0:T(8,128)(2,1)S(1)}, bf16[256,128]{1,0:T(8,128)(2,1)}, u32[]{:S(2)}) copy-start(bf16[256,128]{1,0:T(8,128)(2,1)} %get-tuple-element.8) | copy-start | bytes 196612
  192.2 15.6 %collective-permute-start.7 = (bf16[64,1024]{1,0:T(8,128)(2,1)S(1)}, bf16[64,1024]{1,0:T(8,128)(2,1)S(1)}, u32[]{:S(2)}, u32[]{:S(2)}) collective-permute-start(bf16[64,1024]{1,0:T(8,128)(2,1)S(1)} %fusion.147), channel_id=1, source_target_pairs={{0,1},{1,2},{2,3},{3,0},{128,131},{129,128},{130,129},{131,130},{2... | collective-permute-start | bytes 393224 | tf_op jit(solution)/shard_map/ppermute | solution.py:48

commit v3 on v2

--- a/solution.py
+++ b/solution.py
@@ -1,3 +1,5 @@
+import functools
+
 import jax
 import jax.numpy as jnp
 from jax import lax
@@ -7,6 +9,7 @@
 
 SLOTS = 2
 RUN = 8
+VMEM = 16 << 20
 
 
 def route(images_ref, keys_ref, slots_ref, combine_ref):
@@ -64,31 +67,82 @@
     )
 
 
-def expert(rows, w_in, w_out):
+def apply(count, add, *refs):
+    rows_ref, w_in_ref, w_out_ref = refs[:3]
+    arrived_ref = refs[3] if add else None
+    total_ref, acc_ref = refs[3 + add], refs[-1]
+    step, last = pl.program_id(0), pl.num_programs(0) - 1
     hidden = jax.nn.gelu(
-        jnp.dot(rows, w_in, preferred_element_type=jnp.float32), approximate=True
+        jnp.dot(rows_ref[...], w_in_ref[...], preferred_element_type=jnp.float32),
+        approximate=True,
     ).astype(jnp.bfloat16)
-    return jnp.dot(hidden, w_out, preferred_element_type=jnp.float32)
+    part = jnp.dot(hidden, w_out_ref[...], preferred_element_type=jnp.float32)
+
+    @pl.when(step == 0)
+    def _():
+        acc_ref[...] = part
+
+    @pl.when(step > 0)
+    def _():
+        acc_ref[...] += part
+
+    @pl.when(step == last)
+    def _():
+        total = acc_ref[:count, :]
+        if add:
+            total = total + arrived_ref[...].astype(jnp.float32)
+        total_ref[...] = total.astype(jnp.bfloat16)
+        if rows_ref.shape[0] > count:
+            refs[4 + add][...] = acc_ref[count:, :]
+
+
+def expert(which, rows, w_in, w_out, arrived=None, keep=0):
+    size, width = rows.shape
+    units, count, tile = w_in.shape[2], size - keep, w_in.shape[2] // 4
+    add = arrived is not None
+    out_shape = [jax.ShapeDtypeStruct((count, width), jnp.bfloat16)]
+    if keep:
+        out_shape.append(jax.ShapeDtypeStruct((keep, width), jnp.float32))
+    whole = lambda height: pl.BlockSpec((height, width), lambda j: (0, 0))
+    outs = pl.pallas_call(
+        functools.partial(apply, count, add),
+        grid=(units // tile,),
+        out_shape=out_shape,
+        in_specs=[
+            whole(size),
+            pl.BlockSpec((None, width, tile), lambda j: (which, 0, j)),
+            pl.BlockSpec((None, tile, width), lambda j: (which, j, 0)),
+        ]
+        + [whole(count)] * add,
+        out_specs=[whole(shape.shape[0]) for shape in out_shape],
+        scratch_shapes=[pltpu.VMEM((size, width), jnp.float32)],
+        cost_estimate=pl.CostEstimate(
+            flops=4 * size * width * units,
+            bytes_accessed=4 * width * units,
+            transcendentals=size * units,
+        ),
+        compiler_params=pltpu.CompilerParams(vmem_limit_bytes=VMEM),
+    )(rows, w_in, w_out, *([arrived] if add else []))
+    return outs if keep else outs[0]
 
 
 def rings(owns, w_in, w_out):
-    count, stops, chunks = owns[0].shape[0], lax.axis_size("hid"), range(len(owns))
+    stops, chunks = lax.axis_size("hid"), range(len(owns))
     blocks = [onward(owns[c]) for c in chunks]
-    totals = [expert(blocks[c], w_in[c], w_out[c]).astype(jnp.bfloat16) for c in chunks]
-    for step in range(2, stops):
+    totals, kept, mark = [None for c in chunks], [None for c in chunks], None
+    for step in range(1, stops):
         for c in chunks:
-            both = onward(jnp.concatenate([blocks[c], totals[c]]))
-            if step == stops - 1 and c > 0:
-                both, _ = lax.optimization_barrier((both, totals[c - 1]))
-            blocks[c], total = both[:count], both[count:].astype(jnp.float32)
+            block = blocks[c]
+            if mark is not None:
+                block, _ = lax.optimization_barrier((block, mark))
             if step < stops - 1:
-                totals[c] = (expert(blocks[c], w_in[c], w_out[c]) + total).astype(jnp.bfloat16)
+                blocks[c] = onward(block)
+                mark = expert(c, block, w_in, w_out, totals[c])
             else:
-                last = expert(jnp.concatenate([blocks[c], owns[c]]), w_in[c], w_out[c])
-                totals[c] = (last[:count] + total).astype(jnp.bfloat16)
-                blocks[c] = last[count:]
-    totals = [onward(totals[c]).astype(jnp.float32) for c in chunks]
-    return [(blocks[c] + totals[c]).astype(jnp.bfloat16) for c in chunks]
+                rows = jnp.concatenate([block, owns[c]])
+                mark, kept[c] = expert(c, rows, w_in, w_out, totals[c], owns[c].shape[0])
+            totals[c] = onward(mark)
+    return [(kept[c] + totals[c].astype(jnp.float32)).astype(jnp.bfloat16) for c in chunks]
 
 
 def layer(images_in, slot_keys, w_in, w_out):

time: 229 us -> 232 us (1.013)
  waiting for transfers between devices: 78.5 us -> 49.1 us
  starting transfers between devices: 73.5 us -> 99 us
  matrix products: 19.7 us -> 1.08 us
  Pallas kernels: 2.63 us -> 18 us
  blocking collectives: 51.4 us -> 57.2 us
  local copies, waits for them, and re-layouts: 1.58 us -> 5.92 us
    ppermute x8 -> x12, waiting for transfers between devices: 78.5 us -> 49.1 us  [onward(): return lax.ppermute(value, ('dp', 'hid'), pairs)]
    ppermute x8 -> x12, starting transfers between devices: 73.5 us -> 99 us  [onward(): return lax.ppermute(value, ('dp', 'hid'), pairs)]
    dot_general x6 -> x0, matrix products: 18.7 us -> none  [expert(): return jnp.dot(hidden, w_out, preferred_element_type=jnp.float32)]
    pallas_call x0 -> x6, Pallas kernels: none -> 15.3 us  [expert(): pl.pallas_call(functools.partial(apply, count, add), grid=(units // tile,...]
    all_to_all x2, blocking collectives: 51.4 us -> 57.2 us  [to_owners(): lax.all_to_all(value, ('dp', 'expert', 'hid'), 0, 0, axis_index_groups=te...]
    unnamed x2 -> x8, local copies, waits for them, and re-layouts: 0.01 us -> 4.38 us
  transfers between devices with their start and end apart: 8 -> 12, of which waited for: 5 -> 5; matrix products, arithmetic and copies ran while one was open for 8% -> 0% of each run, Pallas kernels for 0% -> 5%
where the time goes in v3:
time: 232 us; the launch traced here: 231 us
  starting transfers between devices  99 us (43%)
  blocking collectives  57.2 us (25%)
  waiting for transfers between devices  49.1 us (21%)
  Pallas kernels  18 us (8%)
  local copies, waits for them, and re-layouts  5.92 us (3%)
    ppermute x12, starting transfers between devices, onward(): return lax.ppermute(value, ('dp', 'hid'), pairs)  99 us
    all_to_all x2, blocking collectives, to_owners(): lax.all_to_all(value, ('dp', 'expert', 'hid'), 0, 0, axis_index_groups=te...  57.2 us
    ppermute x12, waiting for transfers between devices, onward(): return lax.ppermute(value, ('dp', 'hid'), pairs)  49.1 us
    pallas_call x6, Pallas kernels, expert(): pl.pallas_call(functools.partial(apply, count, add), grid=(units // tile,...  15.3 us
  transfers between devices with their start and end apart: 12, of which 5 were waited for; matrix products, arithmetic and copies ran while one was open for 0% of the time, Pallas kernels for 5%

profile of v3, /device:TPU:8, one launch (start us, length us, event | category | flops | bytes accessed | tf_op | source)
XLA Modules:
  0.0 231.0 jit_solution(12272233121810172039)
XLA Ops:
  0.0 2.6 %shard_map.46 = (bf16[128,1024]{1,0:T(8,128)(2,1)}, bf16[256,128]{1,0:T(8,128)(2,1)}) custom-call(bf16[256,1024]{1,0:T(8,128)(2,1)} %bitcast.7, bf16[1024,128]{1,0:T(8,128)(2,1)} %keys_ref.1), custom_call_target="tpu_custom_call" | custom-call | tf_op jit(solution)/shard_map/pallas_call | solution.py:35
  3.7 32.7 %all_to_all.10 = bf16[32,2,2,1024]{3,2,1,0:T(2,128)(2,1)S(1)} all-to-all(bf16[32,2,2,1024]{3,2,1,0:T(2,128)(2,1)S(1)} %reshape.6), channel_id=1, replica_groups={{0,4,8,12,16,20,24,28,32,36,40,44,48,52,56,60,64,68,72,76,80,84,88,92,9..., dimensions={0} | all-to-all | bytes 524288 | tf_op jit(solution)/shard_map/all_to_all | solution.py:65
  36.6 14.8 %collective-permute-start = (bf16[64,1024]{1,0:T(8,128)(2,1)S(1)}, bf16[64,1024]{1,0:T(8,128)(2,1)S(1)}, u32[]{:S(2)}, u32[]{:S(2)}) collective-permute-start(bf16[64,1024]{1,0:T(8,128)(2,1)S(1)} %reshape_squeeze.6), channel_id=1, source_target_pairs={{0,1},{1,2},{2,3},{3,0},{128,131},{129,128},{130,129},{131,130},{2... | collective-permute-start | bytes 393224 | tf_op jit(solution)/shard_map/ppermute | solution.py:51
  51.5 7.6 %collective-permute-start.2 = (bf16[64,1024]{1,0:T(8,128)(2,1)S(1)}, bf16[64,1024]{1,0:T(8,128)(2,1)S(1)}, u32[]{:S(2)}, u32[]{:S(2)}) collective-permute-start(bf16[64,1024]{1,0:T(8,128)(2,1)S(1)} %reshape_squeeze.7), channel_id=1, source_target_pairs={{0,1},{1,2},{2,3},{3,0},{128,131},{129,128},{130,129},{131,130},{2... | collective-permute-start | bytes 393224 | tf_op jit(solution)/shard_map/ppermute | solution.py:51
  59.1 11.7 %collective-permute-start.1 = (bf16[64,1024]{1,0:T(8,128)(2,1)S(1)}, bf16[64,1024]{1,0:T(8,128)(2,1)S(1)}, u32[]{:S(2)}, u32[]{:S(2)}) collective-permute-start(bf16[64,1024]{1,0:T(8,128)(2,1)S(1)} %collective-permute-done.refs_0_), channel_id=1, source_target_pairs={{0,1},{1,2},{2,3},{3,0},{128,131},{129,128},{130,129},{131,130},{2... | collective-permute-start | bytes 393224 | tf_op jit(solution)/shard_map/ppermute | solution.py:51
  75.1 2.5 %shard_map.47 = bf16[64,1024]{1,0:T(8,128)(2,1)S(1)} custom-call(bf16[64,1024]{1,0:T(8,128)(2,1)S(1)} %collective-permute-done.refs_0_, bf16[2,1024,1024]{2,1,0:T(8,128)(2,1)S(1)} %copy-done, bf16[2,1024,1024]{2,1,0:T(8,128)(2,1)S(1)} %copy-done.2), custom_call_target="tpu_custom_call" | custom-call | flops 268435456 | bytes 4194304 | tf_op jit(solution)/shard_map/pallas_call | solution.py:107
  77.6 12.1 %collective-permute-start.5 = (bf16[64,1024]{1,0:T(8,128)(2,1)S(1)}, bf16[64,1024]{1,0:T(8,128)(2,1)S(1)}, u32[]{:S(2)}, u32[]{:S(2)}) collective-permute-start(bf16[64,1024]{1,0:T(8,128)(2,1)S(1)} %shard_map.47), channel_id=1, source_target_pairs={{0,1},{1,2},{2,3},{3,0},{128,131},{129,128},{130,129},{131,130},{2... | collective-permute-start | bytes 393224 | tf_op jit(solution)/shard_map/ppermute | solution.py:51
  89.7 10.8 %collective-permute-start.4 = (bf16[64,1024]{1,0:T(8,128)(2,1)S(1)}, bf16[64,1024]{1,0:T(8,128)(2,1)S(1)}, u32[]{:S(2)}, u32[]{:S(2)}) collective-permute-start(bf16[64,1024]{1,0:T(8,128)(2,1)S(1)} %collective-permute-done.2.refs_0_), channel_id=1, source_target_pairs={{0,1},{1,2},{2,3},{3,0},{128,131},{129,128},{130,129},{131,130},{2... | collective-permute-start | bytes 393224 | tf_op jit(solution)/shard_map/ppermute | solution.py:51
  100.5 2.5 %shard_map.48 = bf16[64,1024]{1,0:T(8,128)(2,1)S(1)} custom-call(bf16[64,1024]{1,0:T(8,128)(2,1)S(1)} %collective-permute-done.2.refs_0_, bf16[2,1024,1024]{2,1,0:T(8,128)(2,1)S(1)} %copy-done.1, bf16[2,1024,1024]{2,1,0:T(8,128)(2,1)S(1)} %copy-done.2), custom_call_target="tpu_custom_call" | custom-call | flops 268435456 | bytes 4194304 | tf_op jit(solution)/shard_map/pallas_call | solution.py:107
  105.0 4.4 %collective-permute-start.3 = (bf16[64,1024]{1,0:T(8,128)(2,1)S(1)}, bf16[64,1024]{1,0:T(8,128)(2,1)S(1)}, u32[]{:S(2)}, u32[]{:S(2)}) collective-permute-start(bf16[64,1024]{1,0:T(8,128)(2,1)S(1)} %collective-permute-done.1.refs_0_), channel_id=1, source_target_pairs={{0,1},{1,2},{2,3},{3,0},{128,131},{129,128},{130,129},{131,130},{2... | collective-permute-start | bytes 393224 | tf_op jit(solution)/shard_map/ppermute | solution.py:51
  109.3 2.5 %shard_map.49 = bf16[64,1024]{1,0:T(8,128)(2,1)S(1)} custom-call(bf16[64,1024]{1,0:T(8,128)(2,1)S(1)} %collective-permute-done.1.refs_0_, bf16[2,1024,1024]{2,1,0:T(8,128)(2,1)S(1)} %copy-done.1, bf16[2,1024,1024]{2,1,0:T(8,128)(2,1)S(1)} %copy-done.2, bf16[64,1024]{1,0:T(8,128)(2,1)S(1)} %collective-permute-done.5.refs_3_), custom_call_target="tpu_custom_call" | custom-call | flops 268435456 | bytes 4194304 | tf_op jit(solution)/shard_map/pallas_call | solution.py:107
  111.9 12.1 %collective-permute-start.7 = (bf16[64,1024]{1,0:T(8,128)(2,1)S(1)}, bf16[64,1024]{1,0:T(8,128)(2,1)S(1)}, u32[]{:S(2)}, u32[]{:S(2)}) collective-permute-start(bf16[64,1024]{1,0:T(8,128)(2,1)S(1)} %shard_map.49), channel_id=1, source_target_pairs={{0,1},{1,2},{2,3},{3,0},{128,131},{129,128},{130,129},{131,130},{2... | collective-permute-start | bytes 393224 | tf_op jit(solution)/shard_map/ppermute | solution.py:51
  123.9 10.8 %collective-permute-start.9 = (bf16[64,1024]{1,0:T(8,128)(2,1)S(1)}, bf16[64,1024]{1,0:T(8,128)(2,1)S(1)}, u32[]{:S(2)}, u32[]{:S(2)}) collective-permute-start(bf16[64,1024]{1,0:T(8,128)(2,1)S(1)} %collective-permute-done.4.refs_0_), channel_id=1, source_target_pairs={{0,1},{1,2},{2,3},{3,0},{128,131},{129,128},{130,129},{131,130},{2... | collective-permute-start | bytes 393224 | tf_op jit(solution)/shard_map/ppermute | solution.py:51
  134.7 2.5 %shard_map.50 = bf16[64,1024]{1,0:T(8,128)(2,1)S(1)} custom-call(bf16[64,1024]{1,0:T(8,128)(2,1)S(1)} %collective-permute-done.4.refs_0_, bf16[2,1024,1024]{2,1,0:T(8,128)(2,1)S(1)} %copy-done.1, bf16[2,1024,1024]{2,1,0:T(8,128)(2,1)S(1)} %copy-done.2, bf16[64,1024]{1,0:T(8,128)(2,1)S(1)} %collective-permute-done.6.refs_3_), custom_call_target="tpu_custom_call" | custom-call | flops 268435456 | bytes 4194304 | tf_op jit(solution)/shard_map/pallas_call | solution.py:107
  139.2 10.0 %collective-permute-done.7.refs_3_ = bf16[64,1024]{1,0:T(8,128)(2,1)S(1)} collective-permute-done((bf16[64,1024]{1,0:T(8,128)(2,1)S(1)}, bf16[64,1024]{1,0:T(8,128)(2,1)S(1)}, u32[]{:S(2)}, u32[]{:S(2)}) %collective-permute-start.7) | collective-permute-done | bytes 131104 | tf_op jit(solution)/shard_map/ppermute | solution.py:51
  149.2 2.6 %shard_map.51 = (bf16[64,1024]{1,0:T(8,128)(2,1)S(1)}, f32[64,1024]{1,0:T(8,128)S(1)}) custom-call(bf16[128,1024]{1,0:T(8,128)(2,1)S(1)} %pad_maximum_fusion.refs_0_, bf16[2,1024,1024]{2,1,0:T(8,128)(2,1)S(1)} %copy-done.1, bf16[2,1024,1024]{2,1,0:T(8,128)(2,1)S(1)} %copy-done.2, bf16[64,1024]{1,0:T(8,128)(2,1)S(1)} %collective-permute-done.7.refs_3_), custom_call_target="tpu_custom_call" | custom-call | flops 536870912 | bytes 4194304 | tf_op jit(solution)/shard_map/pallas_call | solution.py:107
  151.8 6.2 %collective-permute-done.9 = bf16[64,1024]{1,0:T(8,128)(2,1)S(1)} collective-permute-done((bf16[64,1024]{1,0:T(8,128)(2,1)S(1)}, bf16[64,1024]{1,0:T(8,128)(2,1)S(1)}, u32[]{:S(2)}, u32[]{:S(2)}) %collective-permute-start.9) | collective-permute-done | bytes 131104 | tf_op jit(solution)/shard_map/ppermute | solution.py:51
  158.1 15.0 %collective-permute-done.10.refs_3_ = bf16[64,1024]{1,0:T(8,128)(2,1)S(1)} collective-permute-done((bf16[64,1024]{1,0:T(8,128)(2,1)S(1)}, bf16[64,1024]{1,0:T(8,128)(2,1)S(1)}, u32[]{:S(2)}, u32[]{:S(2)}) %collective-permute-start.10) | collective-permute-done | bytes 131104 | tf_op jit(solution)/shard_map/ppermute | solution.py:51
  173.1 2.6 %shard_map.52 = (bf16[64,1024]{1,0:T(8,128)(2,1)S(1)}, f32[64,1024]{1,0:T(8,128)S(1)}) custom-call(bf16[128,1024]{1,0:T(8,128)(2,1)S(1)} %pad_maximum_fusion.1.refs_0_, bf16[2,1024,1024]{2,1,0:T(8,128)(2,1)S(1)} %copy-done.1, bf16[2,1024,1024]{2,1,0:T(8,128)(2,1)S(1)} %copy-done.2, bf16[64,1024]{1,0:T(8,128)(2,1)S(1)} %collective-permute-done.10.refs_3_), custom_call_target="tpu_custom_call" | custom-call | flops 536870912 | bytes 4194304 | tf_op jit(solution)/shard_map/pallas_call | solution.py:107
  175.8 7.5 %collective-permute-start.11 = (bf16[64,1024]{1,0:T(8,128)(2,1)S(1)}, bf16[64,1024]{1,0:T(8,128)(2,1)S(1)}, u32[]{:S(2)}, u32[]{:S(2)}) collective-permute-start(bf16[64,1024]{1,0:T(8,128)(2,1)S(1)} %get-tuple-element.26), channel_id=1, source_target_pairs={{0,1},{1,2},{2,3},{3,0},{128,131},{129,128},{130,129},{131,130},{2... | collective-permute-start | bytes 393224 | tf_op jit(solution)/shard_map/ppermute | solution.py:51
  183.3 3.5 %collective-permute-start.8 = (bf16[64,1024]{1,0:T(8,128)(2,1)S(1)}, bf16[64,1024]{1,0:T(8,128)(2,1)S(1)}, u32[]{:S(2)}, u32[]{:S(2)}) collective-permute-start(bf16[64,1024]{1,0:T(8,128)(2,1)S(1)} %get-tuple-element.23), channel_id=1, source_target_pairs={{0,1},{1,2},{2,3},{3,0},{128,131},{129,128},{130,129},{131,130},{2... | collective-permute-start | bytes 393224 | tf_op jit(solution)/shard_map/ppermute | solution.py:51
  186.9 10.1 %collective-permute-done.11 = bf16[64,1024]{1,0:T(8,128)(2,1)S(1)} collective-permute-done((bf16[64,1024]{1,0:T(8,128)(2,1)S(1)}, bf16[64,1024]{1,0:T(8,128)(2,1)S(1)}, u32[]{:S(2)}, u32[]{:S(2)}) %collective-permute-start.11) | collective-permute-done | bytes 131104 | tf_op jit(solution)/shard_map/ppermute | solution.py:51
  197.1 7.7 %collective-permute-done.8 = bf16[64,1024]{1,0:T(8,128)(2,1)S(1)} collective-permute-done((bf16[64,1024]{1,0:T(8,128)(2,1)S(1)}, bf16[64,1024]{1,0:T(8,128)(2,1)S(1)}, u32[]{:S(2)}, u32[]{:S(2)}) %collective-permute-start.8) | collective-permute-done | bytes 131104 | tf_op jit(solution)/shard_map/ppermute | solution.py:51
  205.2 24.5 %all_to_all.11 = bf16[32,2,2,1024]{3,2,1,0:T(2,128)(2,1)S(1)} all-to-all(bf16[32,2,2,1024]{3,2,1,0:T(2,128)(2,1)S(1)} %pad_maximum_fusion.2), channel_id=1, replica_groups={{0,4,8,12,16,20,24,28,32,36,40,44,48,52,56,60,64,68,72,76,80,84,88,92,9..., dimensions={0} | all-to-all | bytes 524288 | tf_op jit(solution)/shard_map/all_to_all | solution.py:65
  (30 shorter events, 11.3 us)
Async XLA Ops:
  36.6 22.4 %collective-permute-start = (bf16[64,1024]{1,0:T(8,128)(2,1)S(1)}, bf16[64,1024]{1,0:T(8,128)(2,1)S(1)}, u32[]{:S(2)}, u32[]{:S(2)}) collective-permute-start(bf16[64,1024]{1,0:T(8,128)(2,1)S(1)} %reshape_squeeze.6), channel_id=1, source_target_pairs={{0,1},{1,2},{2,3},{3,0},{128,131},{129,128},{130,129},{131,130},{2... | collective-permute-start | bytes 393224 | tf_op jit(solution)/shard_map/ppermute | solution.py:51
  51.5 38.2 %collective-permute-start.2 = (bf16[64,1024]{1,0:T(8,128)(2,1)S(1)}, bf16[64,1024]{1,0:T(8,128)(2,1)S(1)}, u32[]{:S(2)}, u32[]{:S(2)}) collective-permute-start(bf16[64,1024]{1,0:T(8,128)(2,1)S(1)} %reshape_squeeze.7), channel_id=1, source_target_pairs={{0,1},{1,2},{2,3},{3,0},{128,131},{129,128},{130,129},{131,130},{2... | collective-permute-start | bytes 393224 | tf_op jit(solution)/shard_map/ppermute | solution.py:51
  59.1 45.9 %collective-permute-start.1 = (bf16[64,1024]{1,0:T(8,128)(2,1)S(1)}, bf16[64,1024]{1,0:T(8,128)(2,1)S(1)}, u32[]{:S(2)}, u32[]{:S(2)}) collective-permute-start(bf16[64,1024]{1,0:T(8,128)(2,1)S(1)} %collective-permute-done.refs_0_), channel_id=1, source_target_pairs={{0,1},{1,2},{2,3},{3,0},{128,131},{129,128},{130,129},{131,130},{2... | collective-permute-start | bytes 393224 | tf_op jit(solution)/shard_map/ppermute | solution.py:51
  70.7 2.2 copy-start
  72.9 2.2 copy-start.2
  75.1 25.4 %copy-start.1 = (bf16[2,1024,1024]{2,1,0:T(8,128)(2,1)S(1)}, bf16[2,1024,1024]{2,1,0:T(8,128)(2,1)}, u32[]{:S(2)}) copy-start(bf16[2,1024,1024]{2,1,0:T(8,128)(2,1)} %refs_1_.11) | copy-start | bytes 12582916
  77.6 31.7 %collective-permute-start.5 = (bf16[64,1024]{1,0:T(8,128)(2,1)S(1)}, bf16[64,1024]{1,0:T(8,128)(2,1)S(1)}, u32[]{:S(2)}, u32[]{:S(2)}) collective-permute-start(bf16[64,1024]{1,0:T(8,128)(2,1)S(1)} %shard_map.47), channel_id=1, source_target_pairs={{0,1},{1,2},{2,3},{3,0},{128,131},{129,128},{130,129},{131,130},{2... | collective-permute-start | bytes 393224 | tf_op jit(solution)/shard_map/ppermute | solution.py:51
  89.7 34.2 %collective-permute-start.4 = (bf16[64,1024]{1,0:T(8,128)(2,1)S(1)}, bf16[64,1024]{1,0:T(8,128)(2,1)S(1)}, u32[]{:S(2)}, u32[]{:S(2)}) collective-permute-start(bf16[64,1024]{1,0:T(8,128)(2,1)S(1)} %collective-permute-done.2.refs_0_), channel_id=1, source_target_pairs={{0,1},{1,2},{2,3},{3,0},{128,131},{129,128},{130,129},{131,130},{2... | collective-permute-start | bytes 393224 | tf_op jit(solution)/shard_map/ppermute | solution.py:51
  103.0 31.7 %collective-permute-start.6 = (bf16[64,1024]{1,0:T(8,128)(2,1)S(1)}, bf16[64,1024]{1,0:T(8,128)(2,1)S(1)}, u32[]{:S(2)}, u32[]{:S(2)}) collective-permute-start(bf16[64,1024]{1,0:T(8,128)(2,1)S(1)} %shard_map.48), channel_id=1, source_target_pairs={{0,1},{1,2},{2,3},{3,0},{128,131},{129,128},{130,129},{131,130},{2... | collective-permute-start | bytes 393224 | tf_op jit(solution)/shard_map/ppermute | solution.py:51
  105.0 34.2 %collective-permute-start.3 = (bf16[64,1024]{1,0:T(8,128)(2,1)S(1)}, bf16[64,1024]{1,0:T(8,128)(2,1)S(1)}, u32[]{:S(2)}, u32[]{:S(2)}) collective-permute-start(bf16[64,1024]{1,0:T(8,128)(2,1)S(1)} %collective-permute-done.1.refs_0_), channel_id=1, source_target_pairs={{0,1},{1,2},{2,3},{3,0},{128,131},{129,128},{130,129},{131,130},{2... | collective-permute-start | bytes 393224 | tf_op jit(solution)/shard_map/ppermute | solution.py:51
  111.9 37.3 %collective-permute-start.7 = (bf16[64,1024]{1,0:T(8,128)(2,1)S(1)}, bf16[64,1024]{1,0:T(8,128)(2,1)S(1)}, u32[]{:S(2)}, u32[]{:S(2)}) collective-permute-start(bf16[64,1024]{1,0:T(8,128)(2,1)S(1)} %shard_map.49), channel_id=1, source_target_pairs={{0,1},{1,2},{2,3},{3,0},{128,131},{129,128},{130,129},{131,130},{2... | collective-permute-start | bytes 393224 | tf_op jit(solution)/shard_map/ppermute | solution.py:51
  123.9 34.1 %collective-permute-start.9 = (bf16[64,1024]{1,0:T(8,128)(2,1)S(1)}, bf16[64,1024]{1,0:T(8,128)(2,1)S(1)}, u32[]{:S(2)}, u32[]{:S(2)}) collective-permute-start(bf16[64,1024]{1,0:T(8,128)(2,1)S(1)} %collective-permute-done.4.refs_0_), channel_id=1, source_target_pairs={{0,1},{1,2},{2,3},{3,0},{128,131},{129,128},{130,129},{131,130},{2... | collective-permute-start | bytes 393224 | tf_op jit(solution)/shard_map/ppermute | solution.py:51
  137.3 35.9 %collective-permute-start.10 = (bf16[64,1024]{1,0:T(8,128)(2,1)S(1)}, bf16[64,1024]{1,0:T(8,128)(2,1)S(1)}, u32[]{:S(2)}, u32[]{:S(2)}) collective-permute-start(bf16[64,1024]{1,0:T(8,128)(2,1)S(1)} %shard_map.50), channel_id=1, source_target_pairs={{0,1},{1,2},{2,3},{3,0},{128,131},{129,128},{130,129},{131,130},{2... | collective-permute-start | bytes 393224 | tf_op jit(solution)/shard_map/ppermute | solution.py:51
  158.1 71.8 %copy-start.3 = (bf16[256,128]{1,0:T(8,128)(2,1)S(1)}, bf16[256,128]{1,0:T(8,128)(2,1)}, u32[]{:S(2)}) copy-start(bf16[256,128]{1,0:T(8,128)(2,1)} %get-tuple-element.16) | copy-start | bytes 196612
  175.8 21.2 %collective-permute-start.11 = (bf16[64,1024]{1,0:T(8,128)(2,1)S(1)}, bf16[64,1024]{1,0:T(8,128)(2,1)S(1)}, u32[]{:S(2)}, u32[]{:S(2)}) collective-permute-start(bf16[64,1024]{1,0:T(8,128)(2,1)S(1)} %get-tuple-element.26), channel_id=1, source_target_pairs={{0,1},{1,2},{2,3},{3,0},{128,131},{129,128},{130,129},{131,130},{2... | collective-permute-start | bytes 393224 | tf_op jit(solution)/shard_map/ppermute | solution.py:51
  183.3 21.5 %collective-permute-start.8 = (bf16[64,1024]{1,0:T(8,128)(2,1)S(1)}, bf16[64,1024]{1,0:T(8,128)(2,1)S(1)}, u32[]{:S(2)}, u32[]{:S(2)}) collective-permute-start(bf16[64,1024]{1,0:T(8,128)(2,1)S(1)} %get-tuple-element.23), channel_id=1, source_target_pairs={{0,1},{1,2},{2,3},{3,0},{128,131},{129,128},{130,129},{131,130},{2... | collective-permute-start | bytes 393224 | tf_op jit(solution)/shard_map/ppermute | solution.py:51

commit v4 on v3

--- a/solution.py
+++ b/solution.py
@@ -10,6 +10,10 @@
 SLOTS = 2
 RUN = 8
 VMEM = 16 << 20
+
+
+def in_hbm(value):
+    return pltpu.with_memory_space_constraint(value, pltpu.HBM)
 
 
 def route(images_ref, keys_ref, slots_ref, combine_ref):
@@ -38,8 +42,8 @@
             jax.ShapeDtypeStruct((columns, width), jnp.bfloat16),
             jax.ShapeDtypeStruct((rows, columns), jnp.bfloat16),
         ),
-        compiler_params=pltpu.CompilerParams(vmem_limit_bytes=60 << 20),
-    )(tokens, slot_keys)
+        compiler_params=pltpu.CompilerParams(vmem_limit_bytes=VMEM),
+    )(in_hbm(tokens), in_hbm(slot_keys))
 
 
 def onward(value):
@@ -122,7 +126,7 @@
             transcendentals=size * units,
         ),
         compiler_params=pltpu.CompilerParams(vmem_limit_bytes=VMEM),
-    )(rows, w_in, w_out, *([arrived] if add else []))
+    )(rows, in_hbm(w_in), in_hbm(w_out), *([arrived] if add else []))
     return outs if keep else outs[0]
 
 

time: 232 us -> 228 us (0.983)
  waiting for transfers between devices: 49.1 us -> 39.7 us
  Pallas kernels: 18 us -> 27.1 us
  local copies, waits for them, and re-layouts: 5.92 us -> 0.59 us
  starting transfers between devices: 99 us -> 103 us
    pallas_call x6, Pallas kernels: 15.3 us -> 25.2 us  [expert(): pl.pallas_call(functools.partial(apply, count, add), grid=(units // tile,...]
    ppermute x12, waiting for transfers between devices: 49.1 us -> 39.7 us  [onward(): return lax.ppermute(value, ('dp', 'hid'), pairs)]
    unnamed x8 -> x0, local copies, waits for them, and re-layouts: 4.38 us -> none
    ppermute x12, starting transfers between devices: 99 us -> 103 us  [onward(): return lax.ppermute(value, ('dp', 'hid'), pairs)]
  transfers between devices with their start and end apart: 12 -> 12, of which waited for: 5 -> 4; matrix products, arithmetic and copies ran while one was open for 0% -> 0% of each run, Pallas kernels for 5% -> 9%
where the time goes in v4:
time: 228 us; the launch traced here: 227 us
  starting transfers between devices  103 us (45%)
  blocking collectives  55 us (24%)
  waiting for transfers between devices  39.7 us (17%)
  Pallas kernels  27.1 us (12%)
    ppermute x12, starting transfers between devices, onward(): return lax.ppermute(value, ('dp', 'hid'), pairs)  103 us
    all_to_all x2, blocking collectives, to_owners(): lax.all_to_all(value, ('dp', 'expert', 'hid'), 0, 0, axis_index_groups=te...  55 us
    ppermute x12, waiting for transfers between devices, onward(): return lax.ppermute(value, ('dp', 'hid'), pairs)  39.7 us
    pallas_call x6, Pallas kernels, expert(): pl.pallas_call(functools.partial(apply, count, add), grid=(units // tile,...  25.2 us
  transfers between devices with their start and end apart: 12, of which 4 were waited for; matrix products, arithmetic and copies ran while one was open for 0% of the time, Pallas kernels for 9%

profile of v4, /device:TPU:8, one launch (start us, length us, event | category | flops | bytes accessed | tf_op | source)
XLA Modules:
  0.0 227.1 jit_solution(3774758916606850134)
XLA Ops:
  0.0 1.9 shard_map.46
  2.0 32.7 %all_to_all.10 = bf16[32,2,2,1024]{3,2,1,0:T(2,128)(2,1)S(1)} all-to-all(bf16[32,2,2,1024]{3,2,1,0:T(2,128)(2,1)S(1)} %reshape.6), channel_id=1, replica_groups={{0,4,8,12,16,20,24,28,32,36,40,44,48,52,56,60,64,68,72,76,80,84,88,92,9..., dimensions={0} | all-to-all | bytes 524288 | tf_op jit(solution)/shard_map/all_to_all | solution.py:69
  35.0 14.8 %collective-permute-start = (bf16[64,1024]{1,0:T(8,128)(2,1)S(1)}, bf16[64,1024]{1,0:T(8,128)(2,1)S(1)}, u32[]{:S(2)}, u32[]{:S(2)}) collective-permute-start(bf16[64,1024]{1,0:T(8,128)(2,1)S(1)} %reshape_squeeze.6), channel_id=1, source_target_pairs={{0,1},{1,2},{2,3},{3,0},{128,131},{129,128},{130,129},{131,130},{2... | collective-permute-start | bytes 393224 | tf_op jit(solution)/shard_map/ppermute | solution.py:55
  49.9 7.6 %collective-permute-start.2 = (bf16[64,1024]{1,0:T(8,128)(2,1)S(1)}, bf16[64,1024]{1,0:T(8,128)(2,1)S(1)}, u32[]{:S(2)}, u32[]{:S(2)}) collective-permute-start(bf16[64,1024]{1,0:T(8,128)(2,1)S(1)} %reshape_squeeze.7), channel_id=1, source_target_pairs={{0,1},{1,2},{2,3},{3,0},{128,131},{129,128},{130,129},{131,130},{2... | collective-permute-start | bytes 393224 | tf_op jit(solution)/shard_map/ppermute | solution.py:55
  57.4 11.5 %collective-permute-start.1 = (bf16[64,1024]{1,0:T(8,128)(2,1)S(1)}, bf16[64,1024]{1,0:T(8,128)(2,1)S(1)}, u32[]{:S(2)}, u32[]{:S(2)}) collective-permute-start(bf16[64,1024]{1,0:T(8,128)(2,1)S(1)} %collective-permute-done.refs_0_), channel_id=1, source_target_pairs={{0,1},{1,2},{2,3},{3,0},{128,131},{129,128},{130,129},{131,130},{2... | collective-permute-start | bytes 393224 | tf_op jit(solution)/shard_map/ppermute | solution.py:55
  69.0 4.2 %shard_map.47 = bf16[64,1024]{1,0:T(8,128)(2,1)S(1)} custom-call(bf16[64,1024]{1,0:T(8,128)(2,1)S(1)} %collective-permute-done.refs_0_, bf16[2,1024,1024]{2,1,0:T(8,128)(2,1)} %refs_1_.11, bf16[2,1024,1024]{2,1,0:T(8,128)(2,1)} %refs_2_.11), custom_call_target="tpu_custom_call" | custom-call | flops 268435456 | bytes 4194304 | tf_op jit(solution)/shard_map/pallas_call | solution.py:111
  73.2 12.2 %collective-permute-start.5 = (bf16[64,1024]{1,0:T(8,128)(2,1)S(1)}, bf16[64,1024]{1,0:T(8,128)(2,1)S(1)}, u32[]{:S(2)}, u32[]{:S(2)}) collective-permute-start(bf16[64,1024]{1,0:T(8,128)(2,1)S(1)} %shard_map.47), channel_id=1, source_target_pairs={{0,1},{1,2},{2,3},{3,0},{128,131},{129,128},{130,129},{131,130},{2... | collective-permute-start | bytes 393224 | tf_op jit(solution)/shard_map/ppermute | solution.py:55
  85.4 11.2 %collective-permute-start.4 = (bf16[64,1024]{1,0:T(8,128)(2,1)S(1)}, bf16[64,1024]{1,0:T(8,128)(2,1)S(1)}, u32[]{:S(2)}, u32[]{:S(2)}) collective-permute-start(bf16[64,1024]{1,0:T(8,128)(2,1)S(1)} %collective-permute-done.2.refs_0_), channel_id=1, source_target_pairs={{0,1},{1,2},{2,3},{3,0},{128,131},{129,128},{130,129},{131,130},{2... | collective-permute-start | bytes 393224 | tf_op jit(solution)/shard_map/ppermute | solution.py:55
  96.7 4.2 %shard_map.48 = bf16[64,1024]{1,0:T(8,128)(2,1)S(1)} custom-call(bf16[64,1024]{1,0:T(8,128)(2,1)S(1)} %collective-permute-done.2.refs_0_, bf16[2,1024,1024]{2,1,0:T(8,128)(2,1)} %refs_1_.11, bf16[2,1024,1024]{2,1,0:T(8,128)(2,1)} %refs_2_.11), custom_call_target="tpu_custom_call" | custom-call | flops 268435456 | bytes 4194304 | tf_op jit(solution)/shard_map/pallas_call | solution.py:111
  102.8 3.7 %collective-permute-start.3 = (bf16[64,1024]{1,0:T(8,128)(2,1)S(1)}, bf16[64,1024]{1,0:T(8,128)(2,1)S(1)}, u32[]{:S(2)}, u32[]{:S(2)}) collective-permute-start(bf16[64,1024]{1,0:T(8,128)(2,1)S(1)} %collective-permute-done.1.refs_0_), channel_id=1, source_target_pairs={{0,1},{1,2},{2,3},{3,0},{128,131},{129,128},{130,129},{131,130},{2... | collective-permute-start | bytes 393224 | tf_op jit(solution)/shard_map/ppermute | solution.py:55
  106.5 4.2 %shard_map.49 = bf16[64,1024]{1,0:T(8,128)(2,1)S(1)} custom-call(bf16[64,1024]{1,0:T(8,128)(2,1)S(1)} %collective-permute-done.1.refs_0_, bf16[2,1024,1024]{2,1,0:T(8,128)(2,1)} %refs_1_.11, bf16[2,1024,1024]{2,1,0:T(8,128)(2,1)} %refs_2_.11, bf16[64,1024]{1,0:T(8,128)(2,1)S(1)} %collective-permute-done.5.refs_3_), custom_call_target="tpu_custom_call" | custom-call | flops 268435456 | bytes 4194304 | tf_op jit(solution)/shard_map/pallas_call | solution.py:111
  110.7 12.2 %collective-permute-start.7 = (bf16[64,1024]{1,0:T(8,128)(2,1)S(1)}, bf16[64,1024]{1,0:T(8,128)(2,1)S(1)}, u32[]{:S(2)}, u32[]{:S(2)}) collective-permute-start(bf16[64,1024]{1,0:T(8,128)(2,1)S(1)} %shard_map.49), channel_id=1, source_target_pairs={{0,1},{1,2},{2,3},{3,0},{128,131},{129,128},{130,129},{131,130},{2... | collective-permute-start | bytes 393224 | tf_op jit(solution)/shard_map/ppermute | solution.py:55
  122.9 11.2 %collective-permute-start.9 = (bf16[64,1024]{1,0:T(8,128)(2,1)S(1)}, bf16[64,1024]{1,0:T(8,128)(2,1)S(1)}, u32[]{:S(2)}, u32[]{:S(2)}) collective-permute-start(bf16[64,1024]{1,0:T(8,128)(2,1)S(1)} %collective-permute-done.4.refs_0_), channel_id=1, source_target_pairs={{0,1},{1,2},{2,3},{3,0},{128,131},{129,128},{130,129},{131,130},{2... | collective-permute-start | bytes 393224 | tf_op jit(solution)/shard_map/ppermute | solution.py:55
  134.2 4.2 %shard_map.50 = bf16[64,1024]{1,0:T(8,128)(2,1)S(1)} custom-call(bf16[64,1024]{1,0:T(8,128)(2,1)S(1)} %collective-permute-done.4.refs_0_, bf16[2,1024,1024]{2,1,0:T(8,128)(2,1)} %refs_1_.11, bf16[2,1024,1024]{2,1,0:T(8,128)(2,1)} %refs_2_.11, bf16[64,1024]{1,0:T(8,128)(2,1)S(1)} %collective-permute-done.6.refs_3_), custom_call_target="tpu_custom_call" | custom-call | flops 268435456 | bytes 4194304 | tf_op jit(solution)/shard_map/pallas_call | solution.py:111
  138.4 2.4 %collective-permute-start.10 = (bf16[64,1024]{1,0:T(8,128)(2,1)S(1)}, bf16[64,1024]{1,0:T(8,128)(2,1)S(1)}, u32[]{:S(2)}, u32[]{:S(2)}) collective-permute-start(bf16[64,1024]{1,0:T(8,128)(2,1)S(1)} %shard_map.50), channel_id=1, source_target_pairs={{0,1},{1,2},{2,3},{3,0},{128,131},{129,128},{130,129},{131,130},{2... | collective-permute-start | bytes 393224 | tf_op jit(solution)/shard_map/ppermute | solution.py:55
  140.9 4.3 %shard_map.51 = (bf16[64,1024]{1,0:T(8,128)(2,1)S(1)}, f32[64,1024]{1,0:T(8,128)S(1)}) custom-call(bf16[128,1024]{1,0:T(8,128)(2,1)S(1)} %pad_maximum_fusion.refs_0_, bf16[2,1024,1024]{2,1,0:T(8,128)(2,1)} %refs_1_.11, bf16[2,1024,1024]{2,1,0:T(8,128)(2,1)} %refs_2_.11, bf16[64,1024]{1,0:T(8,128)(2,1)S(1)} %collective-permute-done.7.refs_3_), custom_call_target="tpu_custom_call" | custom-call | flops 536870912 | bytes 4194304 | tf_op jit(solution)/shard_map/pallas_call | solution.py:111
  145.1 11.1 %collective-permute-done.9 = bf16[64,1024]{1,0:T(8,128)(2,1)S(1)} collective-permute-done((bf16[64,1024]{1,0:T(8,128)(2,1)S(1)}, bf16[64,1024]{1,0:T(8,128)(2,1)S(1)}, u32[]{:S(2)}, u32[]{:S(2)}) %collective-permute-start.9) | collective-permute-done | bytes 131104 | tf_op jit(solution)/shard_map/ppermute | solution.py:55
  156.3 10.4 %collective-permute-done.10.refs_3_ = bf16[64,1024]{1,0:T(8,128)(2,1)S(1)} collective-permute-done((bf16[64,1024]{1,0:T(8,128)(2,1)S(1)}, bf16[64,1024]{1,0:T(8,128)(2,1)S(1)}, u32[]{:S(2)}, u32[]{:S(2)}) %collective-permute-start.10) | collective-permute-done | bytes 131104 | tf_op jit(solution)/shard_map/ppermute | solution.py:55
  166.7 4.3 %shard_map.52 = (bf16[64,1024]{1,0:T(8,128)(2,1)S(1)}, f32[64,1024]{1,0:T(8,128)S(1)}) custom-call(bf16[128,1024]{1,0:T(8,128)(2,1)S(1)} %pad_maximum_fusion.1.refs_0_, bf16[2,1024,1024]{2,1,0:T(8,128)(2,1)} %refs_1_.11, bf16[2,1024,1024]{2,1,0:T(8,128)(2,1)} %refs_2_.11, bf16[64,1024]{1,0:T(8,128)(2,1)S(1)} %collective-permute-done.10.refs_3_), custom_call_target="tpu_custom_call" | custom-call | flops 536870912 | bytes 4194304 | tf_op jit(solution)/shard_map/pallas_call | solution.py:111
  171.0 7.5 %collective-permute-start.11 = (bf16[64,1024]{1,0:T(8,128)(2,1)S(1)}, bf16[64,1024]{1,0:T(8,128)(2,1)S(1)}, u32[]{:S(2)}, u32[]{:S(2)}) collective-permute-start(bf16[64,1024]{1,0:T(8,128)(2,1)S(1)} %get-tuple-element.26), channel_id=1, source_target_pairs={{0,1},{1,2},{2,3},{3,0},{128,131},{129,128},{130,129},{131,130},{2... | collective-permute-start | bytes 393224 | tf_op jit(solution)/shard_map/ppermute | solution.py:55
  178.5 6.5 %collective-permute-start.8 = (bf16[64,1024]{1,0:T(8,128)(2,1)S(1)}, bf16[64,1024]{1,0:T(8,128)(2,1)S(1)}, u32[]{:S(2)}, u32[]{:S(2)}) collective-permute-start(bf16[64,1024]{1,0:T(8,128)(2,1)S(1)} %get-tuple-element.23), channel_id=1, source_target_pairs={{0,1},{1,2},{2,3},{3,0},{128,131},{129,128},{130,129},{131,130},{2... | collective-permute-start | bytes 393224 | tf_op jit(solution)/shard_map/ppermute | solution.py:55
  185.0 3.2 %collective-permute-done.11 = bf16[64,1024]{1,0:T(8,128)(2,1)S(1)} collective-permute-done((bf16[64,1024]{1,0:T(8,128)(2,1)S(1)}, bf16[64,1024]{1,0:T(8,128)(2,1)S(1)}, u32[]{:S(2)}, u32[]{:S(2)}) %collective-permute-start.11) | collective-permute-done | bytes 131104 | tf_op jit(solution)/shard_map/ppermute | solution.py:55
  188.2 14.9 %collective-permute-done.8 = bf16[64,1024]{1,0:T(8,128)(2,1)S(1)} collective-permute-done((bf16[64,1024]{1,0:T(8,128)(2,1)S(1)}, bf16[64,1024]{1,0:T(8,128)(2,1)S(1)}, u32[]{:S(2)}, u32[]{:S(2)}) %collective-permute-start.8) | collective-permute-done | bytes 131104 | tf_op jit(solution)/shard_map/ppermute | solution.py:55
  203.6 22.3 %all_to_all.11 = bf16[32,2,2,1024]{3,2,1,0:T(2,128)(2,1)S(1)} all-to-all(bf16[32,2,2,1024]{3,2,1,0:T(2,128)(2,1)S(1)} %pad_maximum_fusion.2), channel_id=1, replica_groups={{0,4,8,12,16,20,24,28,32,36,40,44,48,52,56,60,64,68,72,76,80,84,88,92,9..., dimensions={0} | all-to-all | bytes 524288 | tf_op jit(solution)/shard_map/all_to_all | solution.py:69
  (22 shorter events, 4.0 us)
Async XLA Ops:
  35.0 22.4 %collective-permute-start = (bf16[64,1024]{1,0:T(8,128)(2,1)S(1)}, bf16[64,1024]{1,0:T(8,128)(2,1)S(1)}, u32[]{:S(2)}, u32[]{:S(2)}) collective-permute-start(bf16[64,1024]{1,0:T(8,128)(2,1)S(1)} %reshape_squeeze.6), channel_id=1, source_target_pairs={{0,1},{1,2},{2,3},{3,0},{128,131},{129,128},{130,129},{131,130},{2... | collective-permute-start | bytes 393224 | tf_op jit(solution)/shard_map/ppermute | solution.py:55
  49.9 35.6 %collective-permute-start.2 = (bf16[64,1024]{1,0:T(8,128)(2,1)S(1)}, bf16[64,1024]{1,0:T(8,128)(2,1)S(1)}, u32[]{:S(2)}, u32[]{:S(2)}) collective-permute-start(bf16[64,1024]{1,0:T(8,128)(2,1)S(1)} %reshape_squeeze.7), channel_id=1, source_target_pairs={{0,1},{1,2},{2,3},{3,0},{128,131},{129,128},{130,129},{131,130},{2... | collective-permute-start | bytes 393224 | tf_op jit(solution)/shard_map/ppermute | solution.py:55
  57.4 45.3 %collective-permute-start.1 = (bf16[64,1024]{1,0:T(8,128)(2,1)S(1)}, bf16[64,1024]{1,0:T(8,128)(2,1)S(1)}, u32[]{:S(2)}, u32[]{:S(2)}) collective-permute-start(bf16[64,1024]{1,0:T(8,128)(2,1)S(1)} %collective-permute-done.refs_0_), channel_id=1, source_target_pairs={{0,1},{1,2},{2,3},{3,0},{128,131},{129,128},{130,129},{131,130},{2... | collective-permute-start | bytes 393224 | tf_op jit(solution)/shard_map/ppermute | solution.py:55
  73.2 33.3 %collective-permute-start.5 = (bf16[64,1024]{1,0:T(8,128)(2,1)S(1)}, bf16[64,1024]{1,0:T(8,128)(2,1)S(1)}, u32[]{:S(2)}, u32[]{:S(2)}) collective-permute-start(bf16[64,1024]{1,0:T(8,128)(2,1)S(1)} %shard_map.47), channel_id=1, source_target_pairs={{0,1},{1,2},{2,3},{3,0},{128,131},{129,128},{130,129},{131,130},{2... | collective-permute-start | bytes 393224 | tf_op jit(solution)/shard_map/ppermute | solution.py:55
  85.4 37.5 %collective-permute-start.4 = (bf16[64,1024]{1,0:T(8,128)(2,1)S(1)}, bf16[64,1024]{1,0:T(8,128)(2,1)S(1)}, u32[]{:S(2)}, u32[]{:S(2)}) collective-permute-start(bf16[64,1024]{1,0:T(8,128)(2,1)S(1)} %collective-permute-done.2.refs_0_), channel_id=1, source_target_pairs={{0,1},{1,2},{2,3},{3,0},{128,131},{129,128},{130,129},{131,130},{2... | collective-permute-start | bytes 393224 | tf_op jit(solution)/shard_map/ppermute | solution.py:55
  100.8 33.4 %collective-permute-start.6 = (bf16[64,1024]{1,0:T(8,128)(2,1)S(1)}, bf16[64,1024]{1,0:T(8,128)(2,1)S(1)}, u32[]{:S(2)}, u32[]{:S(2)}) collective-permute-start(bf16[64,1024]{1,0:T(8,128)(2,1)S(1)} %shard_map.48), channel_id=1, source_target_pairs={{0,1},{1,2},{2,3},{3,0},{128,131},{129,128},{130,129},{131,130},{2... | collective-permute-start | bytes 393224 | tf_op jit(solution)/shard_map/ppermute | solution.py:55
  102.8 38.1 %collective-permute-start.3 = (bf16[64,1024]{1,0:T(8,128)(2,1)S(1)}, bf16[64,1024]{1,0:T(8,128)(2,1)S(1)}, u32[]{:S(2)}, u32[]{:S(2)}) collective-permute-start(bf16[64,1024]{1,0:T(8,128)(2,1)S(1)} %collective-permute-done.1.refs_0_), channel_id=1, source_target_pairs={{0,1},{1,2},{2,3},{3,0},{128,131},{129,128},{130,129},{131,130},{2... | collective-permute-start | bytes 393224 | tf_op jit(solution)/shard_map/ppermute | solution.py:55
  110.7 30.2 %collective-permute-start.7 = (bf16[64,1024]{1,0:T(8,128)(2,1)S(1)}, bf16[64,1024]{1,0:T(8,128)(2,1)S(1)}, u32[]{:S(2)}, u32[]{:S(2)}) collective-permute-start(bf16[64,1024]{1,0:T(8,128)(2,1)S(1)} %shard_map.49), channel_id=1, source_target_pairs={{0,1},{1,2},{2,3},{3,0},{128,131},{129,128},{130,129},{131,130},{2... | collective-permute-start | bytes 393224 | tf_op jit(solution)/shard_map/ppermute | solution.py:55
  122.9 33.3 %collective-permute-start.9 = (bf16[64,1024]{1,0:T(8,128)(2,1)S(1)}, bf16[64,1024]{1,0:T(8,128)(2,1)S(1)}, u32[]{:S(2)}, u32[]{:S(2)}) collective-permute-start(bf16[64,1024]{1,0:T(8,128)(2,1)S(1)} %collective-permute-done.4.refs_0_), channel_id=1, source_target_pairs={{0,1},{1,2},{2,3},{3,0},{128,131},{129,128},{130,129},{131,130},{2... | collective-permute-start | bytes 393224 | tf_op jit(solution)/shard_map/ppermute | solution.py:55
  138.4 28.3 %collective-permute-start.10 = (bf16[64,1024]{1,0:T(8,128)(2,1)S(1)}, bf16[64,1024]{1,0:T(8,128)(2,1)S(1)}, u32[]{:S(2)}, u32[]{:S(2)}) collective-permute-start(bf16[64,1024]{1,0:T(8,128)(2,1)S(1)} %shard_map.50), channel_id=1, source_target_pairs={{0,1},{1,2},{2,3},{3,0},{128,131},{129,128},{130,129},{131,130},{2... | collective-permute-start | bytes 393224 | tf_op jit(solution)/shard_map/ppermute | solution.py:55
  171.0 17.2 %collective-permute-start.11 = (bf16[64,1024]{1,0:T(8,128)(2,1)S(1)}, bf16[64,1024]{1,0:T(8,128)(2,1)S(1)}, u32[]{:S(2)}, u32[]{:S(2)}) collective-permute-start(bf16[64,1024]{1,0:T(8,128)(2,1)S(1)} %get-tuple-element.26), channel_id=1, source_target_pairs={{0,1},{1,2},{2,3},{3,0},{128,131},{129,128},{130,129},{131,130},{2... | collective-permute-start | bytes 393224 | tf_op jit(solution)/shard_map/ppermute | solution.py:55
  178.5 24.7 %collective-permute-start.8 = (bf16[64,1024]{1,0:T(8,128)(2,1)S(1)}, bf16[64,1024]{1,0:T(8,128)(2,1)S(1)}, u32[]{:S(2)}, u32[]{:S(2)}) collective-permute-start(bf16[64,1024]{1,0:T(8,128)(2,1)S(1)} %get-tuple-element.23), channel_id=1, source_target_pairs={{0,1},{1,2},{2,3},{3,0},{128,131},{129,128},{130,129},{131,130},{2... | collective-permute-start | bytes 393224 | tf_op jit(solution)/shard_map/ppermute | solution.py:55

commit v5 on v4

--- a/solution.py
+++ b/solution.py
@@ -126,7 +126,7 @@
             transcendentals=size * units,
         ),
         compiler_params=pltpu.CompilerParams(vmem_limit_bytes=VMEM),
-    )(rows, in_hbm(w_in), in_hbm(w_out), *([arrived] if add else []))
+    )(rows, w_in, w_out, *([arrived] if add else []))
     return outs if keep else outs[0]
 
 
@@ -141,7 +141,9 @@
                 block, _ = lax.optimization_barrier((block, mark))
             if step < stops - 1:
                 blocks[c] = onward(block)
-                mark = expert(c, block, w_in, w_out, totals[c])
+                first = step == 1 and c == 0
+                weights = [in_hbm(w) if first else w for w in (w_in, w_out)]
+                mark = expert(c, block, *weights, totals[c])
             else:
                 rows = jnp.concatenate([block, owns[c]])
                 mark, kept[c] = expert(c, rows, w_in, w_out, totals[c], owns[c].shape[0])

time: 228 us -> 229 us (level)
  the two profiles are of different devices: /device:TPU:8 before, /device:TPU:2 now
where the time goes in v5:
time: 229 us; the launch traced here: 228 us
  starting transfers between devices  96.3 us (42%)
  blocking collectives  66.4 us (29%)
  waiting for transfers between devices  44.5 us (19%)
  Pallas kernels  18.9 us (8%)
    ppermute x12, starting transfers between devices, onward(): return lax.ppermute(value, ('dp', 'hid'), pairs)  96.3 us
    all_to_all x2, blocking collectives, to_owners(): lax.all_to_all(value, ('dp', 'expert', 'hid'), 0, 0, axis_index_groups=te...  66.4 us
    ppermute x12, waiting for transfers between devices, onward(): return lax.ppermute(value, ('dp', 'hid'), pairs)  44.5 us
    pallas_call x6, Pallas kernels, expert(): pl.pallas_call(functools.partial(apply, count, add), grid=(units // tile,...  17 us
  transfers between devices with their start and end apart: 12, of which 6 were waited for; matrix products, arithmetic and copies ran while one was open for 0% of the time, Pallas kernels for 6%

profile of v5, /device:TPU:2, one launch (start us, length us, event | category | flops | bytes accessed | tf_op | source)
XLA Modules:
  0.0 228.5 jit_solution(11833770135650328449)
XLA Ops:
  2.0 31.9 %all_to_all.10 = bf16[32,2,2,1024]{3,2,1,0:T(2,128)(2,1)S(1)} all-to-all(bf16[32,2,2,1024]{3,2,1,0:T(2,128)(2,1)S(1)} %reshape.6), channel_id=1, replica_groups={{0,4,8,12,16,20,24,28,32,36,40,44,48,52,56,60,64,68,72,76,80,84,88,92,9..., dimensions={0} | all-to-all | bytes 524288 | tf_op jit(solution)/shard_map/all_to_all | solution.py:69
  34.2 14.1 %collective-permute-start = (bf16[64,1024]{1,0:T(8,128)(2,1)S(1)}, bf16[64,1024]{1,0:T(8,128)(2,1)S(1)}, u32[]{:S(2)}, u32[]{:S(2)}) collective-permute-start(bf16[64,1024]{1,0:T(8,128)(2,1)S(1)} %reshape_squeeze.6), channel_id=1, source_target_pairs={{0,1},{1,2},{2,3},{3,0},{128,131},{129,128},{130,129},{131,130},{2... | collective-permute-start | bytes 393224 | tf_op jit(solution)/shard_map/ppermute | solution.py:55
  48.4 8.4 %collective-permute-start.2 = (bf16[64,1024]{1,0:T(8,128)(2,1)S(1)}, bf16[64,1024]{1,0:T(8,128)(2,1)S(1)}, u32[]{:S(2)}, u32[]{:S(2)}) collective-permute-start(bf16[64,1024]{1,0:T(8,128)(2,1)S(1)} %reshape_squeeze.7), channel_id=1, source_target_pairs={{0,1},{1,2},{2,3},{3,0},{128,131},{129,128},{130,129},{131,130},{2... | collective-permute-start | bytes 393224 | tf_op jit(solution)/shard_map/ppermute | solution.py:55
  56.7 11.2 %collective-permute-start.1 = (bf16[64,1024]{1,0:T(8,128)(2,1)S(1)}, bf16[64,1024]{1,0:T(8,128)(2,1)S(1)}, u32[]{:S(2)}, u32[]{:S(2)}) collective-permute-start(bf16[64,1024]{1,0:T(8,128)(2,1)S(1)} %collective-permute-done.refs_0_), channel_id=1, source_target_pairs={{0,1},{1,2},{2,3},{3,0},{128,131},{129,128},{130,129},{131,130},{2... | collective-permute-start | bytes 393224 | tf_op jit(solution)/shard_map/ppermute | solution.py:55
  67.9 4.2 %shard_map.47 = bf16[64,1024]{1,0:T(8,128)(2,1)S(1)} custom-call(bf16[64,1024]{1,0:T(8,128)(2,1)S(1)} %collective-permute-done.refs_0_, bf16[2,1024,1024]{2,1,0:T(8,128)(2,1)} %refs_1_.11, bf16[2,1024,1024]{2,1,0:T(8,128)(2,1)} %refs_2_.11), custom_call_target="tpu_custom_call" | custom-call | flops 268435456 | bytes 4194304 | tf_op jit(solution)/shard_map/pallas_call | solution.py:111
  72.1 12.1 %collective-permute-start.5 = (bf16[64,1024]{1,0:T(8,128)(2,1)S(1)}, bf16[64,1024]{1,0:T(8,128)(2,1)S(1)}, u32[]{:S(2)}, u32[]{:S(2)}) collective-permute-start(bf16[64,1024]{1,0:T(8,128)(2,1)S(1)} %shard_map.47), channel_id=1, source_target_pairs={{0,1},{1,2},{2,3},{3,0},{128,131},{129,128},{130,129},{131,130},{2... | collective-permute-start | bytes 393224 | tf_op jit(solution)/shard_map/ppermute | solution.py:55
  84.2 11.0 %collective-permute-start.4 = (bf16[64,1024]{1,0:T(8,128)(2,1)S(1)}, bf16[64,1024]{1,0:T(8,128)(2,1)S(1)}, u32[]{:S(2)}, u32[]{:S(2)}) collective-permute-start(bf16[64,1024]{1,0:T(8,128)(2,1)S(1)} %collective-permute-done.2.refs_0_), channel_id=1, source_target_pairs={{0,1},{1,2},{2,3},{3,0},{128,131},{129,128},{130,129},{131,130},{2... | collective-permute-start | bytes 393224 | tf_op jit(solution)/shard_map/ppermute | solution.py:55
  95.2 2.5 %shard_map.48 = bf16[64,1024]{1,0:T(8,128)(2,1)S(1)} custom-call(bf16[64,1024]{1,0:T(8,128)(2,1)S(1)} %collective-permute-done.2.refs_0_, bf16[2,1024,1024]{2,1,0:T(8,128)(2,1)S(1)} %copy-done, bf16[2,1024,1024]{2,1,0:T(8,128)(2,1)S(1)} %copy-done.1), custom_call_target="tpu_custom_call" | custom-call | flops 268435456 | bytes 4194304 | tf_op jit(solution)/shard_map/pallas_call | solution.py:111
  99.7 4.1 %collective-permute-start.3 = (bf16[64,1024]{1,0:T(8,128)(2,1)S(1)}, bf16[64,1024]{1,0:T(8,128)(2,1)S(1)}, u32[]{:S(2)}, u32[]{:S(2)}) collective-permute-start(bf16[64,1024]{1,0:T(8,128)(2,1)S(1)} %collective-permute-done.1.refs_0_), channel_id=1, source_target_pairs={{0,1},{1,2},{2,3},{3,0},{128,131},{129,128},{130,129},{131,130},{2... | collective-permute-start | bytes 393224 | tf_op jit(solution)/shard_map/ppermute | solution.py:55
  103.8 4.3 %collective-permute-done.5.refs_3_ = bf16[64,1024]{1,0:T(8,128)(2,1)S(1)} collective-permute-done((bf16[64,1024]{1,0:T(8,128)(2,1)S(1)}, bf16[64,1024]{1,0:T(8,128)(2,1)S(1)}, u32[]{:S(2)}, u32[]{:S(2)}) %collective-permute-start.5) | collective-permute-done | bytes 131104 | tf_op jit(solution)/shard_map/ppermute | solution.py:55
  108.0 2.5 %shard_map.49 = bf16[64,1024]{1,0:T(8,128)(2,1)S(1)} custom-call(bf16[64,1024]{1,0:T(8,128)(2,1)S(1)} %collective-permute-done.1.refs_0_, bf16[2,1024,1024]{2,1,0:T(8,128)(2,1)S(1)} %copy-done, bf16[2,1024,1024]{2,1,0:T(8,128)(2,1)S(1)} %copy-done.1, bf16[64,1024]{1,0:T(8,128)(2,1)S(1)} %collective-permute-done.5.refs_3_), custom_call_target="tpu_custom_call" | custom-call | flops 268435456 | bytes 4194304 | tf_op jit(solution)/shard_map/pallas_call | solution.py:111
  110.5 7.9 %collective-permute-start.7 = (bf16[64,1024]{1,0:T(8,128)(2,1)S(1)}, bf16[64,1024]{1,0:T(8,128)(2,1)S(1)}, u32[]{:S(2)}, u32[]{:S(2)}) collective-permute-start(bf16[64,1024]{1,0:T(8,128)(2,1)S(1)} %shard_map.49), channel_id=1, source_target_pairs={{0,1},{1,2},{2,3},{3,0},{128,131},{129,128},{130,129},{131,130},{2... | collective-permute-start | bytes 393224 | tf_op jit(solution)/shard_map/ppermute | solution.py:55
  118.4 11.0 %collective-permute-start.9 = (bf16[64,1024]{1,0:T(8,128)(2,1)S(1)}, bf16[64,1024]{1,0:T(8,128)(2,1)S(1)}, u32[]{:S(2)}, u32[]{:S(2)}) collective-permute-start(bf16[64,1024]{1,0:T(8,128)(2,1)S(1)} %collective-permute-done.4.refs_0_), channel_id=1, source_target_pairs={{0,1},{1,2},{2,3},{3,0},{128,131},{129,128},{130,129},{131,130},{2... | collective-permute-start | bytes 393224 | tf_op jit(solution)/shard_map/ppermute | solution.py:55
  129.5 2.5 %shard_map.50 = bf16[64,1024]{1,0:T(8,128)(2,1)S(1)} custom-call(bf16[64,1024]{1,0:T(8,128)(2,1)S(1)} %collective-permute-done.4.refs_0_, bf16[2,1024,1024]{2,1,0:T(8,128)(2,1)S(1)} %copy-done, bf16[2,1024,1024]{2,1,0:T(8,128)(2,1)S(1)} %copy-done.1, bf16[64,1024]{1,0:T(8,128)(2,1)S(1)} %collective-permute-done.6.refs_3_), custom_call_target="tpu_custom_call" | custom-call | flops 268435456 | bytes 4194304 | tf_op jit(solution)/shard_map/pallas_call | solution.py:111
  134.0 12.3 %collective-permute-done.7.refs_3_ = bf16[64,1024]{1,0:T(8,128)(2,1)S(1)} collective-permute-done((bf16[64,1024]{1,0:T(8,128)(2,1)S(1)}, bf16[64,1024]{1,0:T(8,128)(2,1)S(1)}, u32[]{:S(2)}, u32[]{:S(2)}) %collective-permute-start.7) | collective-permute-done | bytes 131104 | tf_op jit(solution)/shard_map/ppermute | solution.py:55
  146.3 2.6 %shard_map.51 = (bf16[64,1024]{1,0:T(8,128)(2,1)S(1)}, f32[64,1024]{1,0:T(8,128)S(1)}) custom-call(bf16[128,1024]{1,0:T(8,128)(2,1)S(1)} %pad_maximum_fusion.refs_0_, bf16[2,1024,1024]{2,1,0:T(8,128)(2,1)S(1)} %copy-done, bf16[2,1024,1024]{2,1,0:T(8,128)(2,1)S(1)} %copy-done.1, bf16[64,1024]{1,0:T(8,128)(2,1)S(1)} %collective-permute-done.7.refs_3_), custom_call_target="tpu_custom_call" | custom-call | flops 536870912 | bytes 4194304 | tf_op jit(solution)/shard_map/pallas_call | solution.py:111
  149.0 8.3 %collective-permute-done.9 = bf16[64,1024]{1,0:T(8,128)(2,1)S(1)} collective-permute-done((bf16[64,1024]{1,0:T(8,128)(2,1)S(1)}, bf16[64,1024]{1,0:T(8,128)(2,1)S(1)}, u32[]{:S(2)}, u32[]{:S(2)}) %collective-permute-start.9) | collective-permute-done | bytes 131104 | tf_op jit(solution)/shard_map/ppermute | solution.py:55
  157.3 6.0 %collective-permute-done.10.refs_3_ = bf16[64,1024]{1,0:T(8,128)(2,1)S(1)} collective-permute-done((bf16[64,1024]{1,0:T(8,128)(2,1)S(1)}, bf16[64,1024]{1,0:T(8,128)(2,1)S(1)}, u32[]{:S(2)}, u32[]{:S(2)}) %collective-permute-start.10) | collective-permute-done | bytes 131104 | tf_op jit(solution)/shard_map/ppermute | solution.py:55
  163.3 2.6 %shard_map.52 = (bf16[64,1024]{1,0:T(8,128)(2,1)S(1)}, f32[64,1024]{1,0:T(8,128)S(1)}) custom-call(bf16[128,1024]{1,0:T(8,128)(2,1)S(1)} %pad_maximum_fusion.1.refs_0_, bf16[2,1024,1024]{2,1,0:T(8,128)(2,1)S(1)} %copy-done, bf16[2,1024,1024]{2,1,0:T(8,128)(2,1)S(1)} %copy-done.1, bf16[64,1024]{1,0:T(8,128)(2,1)S(1)} %collective-permute-done.10.refs_3_), custom_call_target="tpu_custom_call" | custom-call | flops 536870912 | bytes 4194304 | tf_op jit(solution)/shard_map/pallas_call | solution.py:111
  166.0 5.9 %collective-permute-start.11 = (bf16[64,1024]{1,0:T(8,128)(2,1)S(1)}, bf16[64,1024]{1,0:T(8,128)(2,1)S(1)}, u32[]{:S(2)}, u32[]{:S(2)}) collective-permute-start(bf16[64,1024]{1,0:T(8,128)(2,1)S(1)} %get-tuple-element.26), channel_id=1, source_target_pairs={{0,1},{1,2},{2,3},{3,0},{128,131},{129,128},{130,129},{131,130},{2... | collective-permute-start | bytes 393224 | tf_op jit(solution)/shard_map/ppermute | solution.py:55
  171.9 6.8 %collective-permute-start.8 = (bf16[64,1024]{1,0:T(8,128)(2,1)S(1)}, bf16[64,1024]{1,0:T(8,128)(2,1)S(1)}, u32[]{:S(2)}, u32[]{:S(2)}) collective-permute-start(bf16[64,1024]{1,0:T(8,128)(2,1)S(1)} %get-tuple-element.23), channel_id=1, source_target_pairs={{0,1},{1,2},{2,3},{3,0},{128,131},{129,128},{130,129},{131,130},{2... | collective-permute-start | bytes 393224 | tf_op jit(solution)/shard_map/ppermute | solution.py:55
  178.7 3.2 %collective-permute-done.11 = bf16[64,1024]{1,0:T(8,128)(2,1)S(1)} collective-permute-done((bf16[64,1024]{1,0:T(8,128)(2,1)S(1)}, bf16[64,1024]{1,0:T(8,128)(2,1)S(1)}, u32[]{:S(2)}, u32[]{:S(2)}) %collective-permute-start.11) | collective-permute-done | bytes 131104 | tf_op jit(solution)/shard_map/ppermute | solution.py:55
  182.1 10.3 %collective-permute-done.8 = bf16[64,1024]{1,0:T(8,128)(2,1)S(1)} collective-permute-done((bf16[64,1024]{1,0:T(8,128)(2,1)S(1)}, bf16[64,1024]{1,0:T(8,128)(2,1)S(1)}, u32[]{:S(2)}, u32[]{:S(2)}) %collective-permute-start.8) | collective-permute-done | bytes 131104 | tf_op jit(solution)/shard_map/ppermute | solution.py:55
  192.8 34.5 %all_to_all.11 = bf16[32,2,2,1024]{3,2,1,0:T(2,128)(2,1)S(1)} all-to-all(bf16[32,2,2,1024]{3,2,1,0:T(2,128)(2,1)S(1)} %pad_maximum_fusion.2), channel_id=1, replica_groups={{0,4,8,12,16,20,24,28,32,36,40,44,48,52,56,60,64,68,72,76,80,84,88,92,9..., dimensions={0} | all-to-all | bytes 524288 | tf_op jit(solution)/shard_map/all_to_all | solution.py:69
  (26 shorter events, 7.9 us)
Async XLA Ops:
  34.2 22.6 %collective-permute-start = (bf16[64,1024]{1,0:T(8,128)(2,1)S(1)}, bf16[64,1024]{1,0:T(8,128)(2,1)S(1)}, u32[]{:S(2)}, u32[]{:S(2)}) collective-permute-start(bf16[64,1024]{1,0:T(8,128)(2,1)S(1)} %reshape_squeeze.6), channel_id=1, source_target_pairs={{0,1},{1,2},{2,3},{3,0},{128,131},{129,128},{130,129},{131,130},{2... | collective-permute-start | bytes 393224 | tf_op jit(solution)/shard_map/ppermute | solution.py:55
  48.3 46.9 %copy-start = (bf16[2,1024,1024]{2,1,0:T(8,128)(2,1)S(1)}, bf16[2,1024,1024]{2,1,0:T(8,128)(2,1)}, u32[]{:S(2)}) copy-start(bf16[2,1024,1024]{2,1,0:T(8,128)(2,1)} %refs_1_.11) | copy-start | bytes 12582916
  48.4 46.9 %copy-start.1 = (bf16[2,1024,1024]{2,1,0:T(8,128)(2,1)S(1)}, bf16[2,1024,1024]{2,1,0:T(8,128)(2,1)}, u32[]{:S(2)}) copy-start(bf16[2,1024,1024]{2,1,0:T(8,128)(2,1)} %refs_2_.11) | copy-start | bytes 12582916
  48.4 35.8 %collective-permute-start.2 = (bf16[64,1024]{1,0:T(8,128)(2,1)S(1)}, bf16[64,1024]{1,0:T(8,128)(2,1)S(1)}, u32[]{:S(2)}, u32[]{:S(2)}) collective-permute-start(bf16[64,1024]{1,0:T(8,128)(2,1)S(1)} %reshape_squeeze.7), channel_id=1, source_target_pairs={{0,1},{1,2},{2,3},{3,0},{128,131},{129,128},{130,129},{131,130},{2... | collective-permute-start | bytes 393224 | tf_op jit(solution)/shard_map/ppermute | solution.py:55
  56.7 42.9 %collective-permute-start.1 = (bf16[64,1024]{1,0:T(8,128)(2,1)S(1)}, bf16[64,1024]{1,0:T(8,128)(2,1)S(1)}, u32[]{:S(2)}, u32[]{:S(2)}) collective-permute-start(bf16[64,1024]{1,0:T(8,128)(2,1)S(1)} %collective-permute-done.refs_0_), channel_id=1, source_target_pairs={{0,1},{1,2},{2,3},{3,0},{128,131},{129,128},{130,129},{131,130},{2... | collective-permute-start | bytes 393224 | tf_op jit(solution)/shard_map/ppermute | solution.py:55
  72.1 36.0 %collective-permute-start.5 = (bf16[64,1024]{1,0:T(8,128)(2,1)S(1)}, bf16[64,1024]{1,0:T(8,128)(2,1)S(1)}, u32[]{:S(2)}, u32[]{:S(2)}) collective-permute-start(bf16[64,1024]{1,0:T(8,128)(2,1)S(1)} %shard_map.47), channel_id=1, source_target_pairs={{0,1},{1,2},{2,3},{3,0},{128,131},{129,128},{130,129},{131,130},{2... | collective-permute-start | bytes 393224 | tf_op jit(solution)/shard_map/ppermute | solution.py:55
  84.2 34.2 %collective-permute-start.4 = (bf16[64,1024]{1,0:T(8,128)(2,1)S(1)}, bf16[64,1024]{1,0:T(8,128)(2,1)S(1)}, u32[]{:S(2)}, u32[]{:S(2)}) collective-permute-start(bf16[64,1024]{1,0:T(8,128)(2,1)S(1)} %collective-permute-done.2.refs_0_), channel_id=1, source_target_pairs={{0,1},{1,2},{2,3},{3,0},{128,131},{129,128},{130,129},{131,130},{2... | collective-permute-start | bytes 393224 | tf_op jit(solution)/shard_map/ppermute | solution.py:55
  97.7 31.7 %collective-permute-start.6 = (bf16[64,1024]{1,0:T(8,128)(2,1)S(1)}, bf16[64,1024]{1,0:T(8,128)(2,1)S(1)}, u32[]{:S(2)}, u32[]{:S(2)}) collective-permute-start(bf16[64,1024]{1,0:T(8,128)(2,1)S(1)} %shard_map.48), channel_id=1, source_target_pairs={{0,1},{1,2},{2,3},{3,0},{128,131},{129,128},{130,129},{131,130},{2... | collective-permute-start | bytes 393224 | tf_op jit(solution)/shard_map/ppermute | solution.py:55
  99.7 34.2 %collective-permute-start.3 = (bf16[64,1024]{1,0:T(8,128)(2,1)S(1)}, bf16[64,1024]{1,0:T(8,128)(2,1)S(1)}, u32[]{:S(2)}, u32[]{:S(2)}) collective-permute-start(bf16[64,1024]{1,0:T(8,128)(2,1)S(1)} %collective-permute-done.1.refs_0_), channel_id=1, source_target_pairs={{0,1},{1,2},{2,3},{3,0},{128,131},{129,128},{130,129},{131,130},{2... | collective-permute-start | bytes 393224 | tf_op jit(solution)/shard_map/ppermute | solution.py:55
  110.5 35.8 %collective-permute-start.7 = (bf16[64,1024]{1,0:T(8,128)(2,1)S(1)}, bf16[64,1024]{1,0:T(8,128)(2,1)S(1)}, u32[]{:S(2)}, u32[]{:S(2)}) collective-permute-start(bf16[64,1024]{1,0:T(8,128)(2,1)S(1)} %shard_map.49), channel_id=1, source_target_pairs={{0,1},{1,2},{2,3},{3,0},{128,131},{129,128},{130,129},{131,130},{2... | collective-permute-start | bytes 393224 | tf_op jit(solution)/shard_map/ppermute | solution.py:55
  118.4 38.9 %collective-permute-start.9 = (bf16[64,1024]{1,0:T(8,128)(2,1)S(1)}, bf16[64,1024]{1,0:T(8,128)(2,1)S(1)}, u32[]{:S(2)}, u32[]{:S(2)}) collective-permute-start(bf16[64,1024]{1,0:T(8,128)(2,1)S(1)} %collective-permute-done.4.refs_0_), channel_id=1, source_target_pairs={{0,1},{1,2},{2,3},{3,0},{128,131},{129,128},{130,129},{131,130},{2... | collective-permute-start | bytes 393224 | tf_op jit(solution)/shard_map/ppermute | solution.py:55
  132.0 31.3 %collective-permute-start.10 = (bf16[64,1024]{1,0:T(8,128)(2,1)S(1)}, bf16[64,1024]{1,0:T(8,128)(2,1)S(1)}, u32[]{:S(2)}, u32[]{:S(2)}) collective-permute-start(bf16[64,1024]{1,0:T(8,128)(2,1)S(1)} %shard_map.50), channel_id=1, source_target_pairs={{0,1},{1,2},{2,3},{3,0},{128,131},{129,128},{130,129},{131,130},{2... | collective-permute-start | bytes 393224 | tf_op jit(solution)/shard_map/ppermute | solution.py:55
  166.0 16.0 %collective-permute-start.11 = (bf16[64,1024]{1,0:T(8,128)(2,1)S(1)}, bf16[64,1024]{1,0:T(8,128)(2,1)S(1)}, u32[]{:S(2)}, u32[]{:S(2)}) collective-permute-start(bf16[64,1024]{1,0:T(8,128)(2,1)S(1)} %get-tuple-element.26), channel_id=1, source_target_pairs={{0,1},{1,2},{2,3},{3,0},{128,131},{129,128},{130,129},{131,130},{2... | collective-permute-start | bytes 393224 | tf_op jit(solution)/shard_map/ppermute | solution.py:55
  171.9 20.4 %collective-permute-start.8 = (bf16[64,1024]{1,0:T(8,128)(2,1)S(1)}, bf16[64,1024]{1,0:T(8,128)(2,1)S(1)}, u32[]{:S(2)}, u32[]{:S(2)}) collective-permute-start(bf16[64,1024]{1,0:T(8,128)(2,1)S(1)} %get-tuple-element.23), channel_id=1, source_target_pairs={{0,1},{1,2},{2,3},{3,0},{128,131},{129,128},{130,129},{131,130},{2... | collective-permute-start | bytes 393224 | tf_op jit(solution)/shard_map/ppermute | solution.py:55

commit v6 on v2

--- a/solution.py
+++ b/solution.py
@@ -7,6 +7,10 @@
 
 SLOTS = 2
 RUN = 8
+
+
+def in_hbm(value):
+    return pltpu.with_memory_space_constraint(value, pltpu.HBM)
 
 
 def route(images_ref, keys_ref, slots_ref, combine_ref):
@@ -35,8 +39,8 @@
             jax.ShapeDtypeStruct((columns, width), jnp.bfloat16),
             jax.ShapeDtypeStruct((rows, columns), jnp.bfloat16),
         ),
-        compiler_params=pltpu.CompilerParams(vmem_limit_bytes=60 << 20),
-    )(tokens, slot_keys)
+        compiler_params=pltpu.CompilerParams(vmem_limit_bytes=16 << 20),
+    )(in_hbm(tokens), in_hbm(slot_keys))
 
 
 def onward(value):

time: 229 us -> 226 us (0.987)
  the two profiles are of different devices: /device:TPU:8 before, /device:TPU:24 now
where the time goes in v6:
time: 226 us; the launch traced here: 225 us
  waiting for transfers between devices  74.4 us (33%)
  starting transfers between devices  70.3 us (31%)
  blocking collectives  57.7 us (26%)
  matrix products  19.7 us (9%)
    ppermute x8, waiting for transfers between devices, onward(): return lax.ppermute(value, ('dp', 'hid'), pairs)  74.4 us
    ppermute x8, starting transfers between devices, onward(): return lax.ppermute(value, ('dp', 'hid'), pairs)  70.3 us
    all_to_all x2, blocking collectives, to_owners(): lax.all_to_all(value, ('dp', 'expert', 'hid'), 0, 0, axis_index_groups=te...  57.7 us
    dot_general x6, matrix products, expert(): return jnp.dot(hidden, w_out, preferred_element_type=jnp.float32)  18.6 us
  transfers between devices with their start and end apart: 8, of which 5 were waited for; matrix products, arithmetic and copies ran while one was open for 8% of the time, Pallas kernels for 0%

profile of v6, /device:TPU:24, one launch (start us, length us, event | category | flops | bytes accessed | tf_op | source)
XLA Modules:
  0.0 225.5 jit_solution(2784606364023198657)
XLA Ops:
  0.0 1.9 shard_map.46
  2.0 32.7 %all_to_all.10 = bf16[32,2,2,1024]{3,2,1,0:T(2,128)(2,1)S(1)} all-to-all(bf16[32,2,2,1024]{3,2,1,0:T(2,128)(2,1)S(1)} %reshape.6), channel_id=1, replica_groups={{0,4,8,12,16,20,24,28,32,36,40,44,48,52,56,60,64,68,72,76,80,84,88,92,9..., dimensions={0} | all-to-all | bytes 524288 | tf_op jit(solution)/shard_map/all_to_all | solution.py:66
  35.0 14.8 %collective-permute-start = (bf16[64,1024]{1,0:T(8,128)(2,1)S(1)}, bf16[64,1024]{1,0:T(8,128)(2,1)S(1)}, u32[]{:S(2)}, u32[]{:S(2)}) collective-permute-start(bf16[64,1024]{1,0:T(8,128)(2,1)S(1)} %reshape_squeeze.6), channel_id=1, source_target_pairs={{0,1},{1,2},{2,3},{3,0},{128,131},{129,128},{130,129},{131,130},{2... | collective-permute-start | bytes 393224 | tf_op jit(solution)/shard_map/ppermute | solution.py:52
  49.9 7.6 %collective-permute-start.4 = (bf16[64,1024]{1,0:T(8,128)(2,1)S(1)}, bf16[64,1024]{1,0:T(8,128)(2,1)S(1)}, u32[]{:S(2)}, u32[]{:S(2)}) collective-permute-start(bf16[64,1024]{1,0:T(8,128)(2,1)S(1)} %reshape_squeeze.7), channel_id=1, source_target_pairs={{0,1},{1,2},{2,3},{3,0},{128,131},{129,128},{130,129},{131,130},{2... | collective-permute-start | bytes 393224 | tf_op jit(solution)/shard_map/ppermute | solution.py:52
  57.4 3.1 %fusion.37 = bf16[64,1024]{1,0:T(8,128)(2,1)S(1)} fusion(bf16[2,1024,1024]{2,1,0:T(8,128)(2,1)} %param.7, bf16[64,1024]{1,0:T(8,128)(2,1)S(1)} %collective-permute-done, bf16[2,1024,1024]{2,1,0:T(8,128)(2,1)} %param.6), kind=kOutput, calls=%fused_computation.38 | convolution fusion | flops 269090816 | bytes 4456448 | tf_op jit(solution)/shard_map/dot_general | solution.py:75
  60.6 11.6 %collective-permute-start.1 = (bf16[128,1024]{1,0:T(8,128)(2,1)S(1)}, bf16[128,1024]{1,0:T(8,128)(2,1)S(1)}, u32[]{:S(2)}, u32[]{:S(2)}) collective-permute-start(bf16[128,1024]{1,0:T(8,128)(2,1)S(1)} %pad_maximum_fusion), channel_id=1, source_target_pairs={{0,1},{1,2},{2,3},{3,0},{128,131},{129,128},{130,129},{131,130},{2... | collective-permute-start | bytes 786440 | tf_op jit(solution)/shard_map/ppermute | solution.py:52
  72.2 2.3 %collective-permute-done.4 = bf16[64,1024]{1,0:T(8,128)(2,1)S(1)} collective-permute-done((bf16[64,1024]{1,0:T(8,128)(2,1)S(1)}, bf16[64,1024]{1,0:T(8,128)(2,1)S(1)}, u32[]{:S(2)}, u32[]{:S(2)}) %collective-permute-start.4) | collective-permute-done | bytes 131104 | tf_op jit(solution)/shard_map/ppermute | solution.py:52
  74.5 3.1 %fusion.40 = bf16[64,1024]{1,0:T(8,128)(2,1)S(1)} fusion(bf16[2,1024,1024]{2,1,0:T(8,128)(2,1)} %param.7, bf16[64,1024]{1,0:T(8,128)(2,1)S(1)} %collective-permute-done.4, bf16[2,1024,1024]{2,1,0:T(8,128)(2,1)} %param.6), kind=kOutput, calls=%fused_computation.39 | convolution fusion | flops 269090816 | bytes 4456448 | tf_op jit(solution)/shard_map/dot_general | solution.py:75
  77.7 9.9 %collective-permute-start.5 = (bf16[128,1024]{1,0:T(8,128)(2,1)S(1)}, bf16[128,1024]{1,0:T(8,128)(2,1)S(1)}, u32[]{:S(2)}, u32[]{:S(2)}) collective-permute-start(bf16[128,1024]{1,0:T(8,128)(2,1)S(1)} %pad_maximum_fusion.2), channel_id=1, source_target_pairs={{0,1},{1,2},{2,3},{3,0},{128,131},{129,128},{130,129},{131,130},{2... | collective-permute-start | bytes 786440 | tf_op jit(solution)/shard_map/ppermute | solution.py:52
  87.5 38.4 %collective-permute-done.1 = bf16[128,1024]{1,0:T(8,128)(2,1)S(1)} collective-permute-done((bf16[128,1024]{1,0:T(8,128)(2,1)S(1)}, bf16[128,1024]{1,0:T(8,128)(2,1)S(1)}, u32[]{:S(2)}, u32[]{:S(2)}) %collective-permute-start.1) | collective-permute-done | bytes 262176 | tf_op jit(solution)/shard_map/ppermute | solution.py:52
  125.9 3.1 %fusion.104 = bf16[64,1024]{1,0:T(8,128)(2,1)S(1)} fusion(bf16[2,1024,1024]{2,1,0:T(8,128)(2,1)} %param.7, bf16[2,1024,1024]{2,1,0:T(8,128)(2,1)} %param.6, bf16[128,1024]{1,0:T(8,128)(2,1)S(1)} %collective-permute-done.1), kind=kOutput, calls=%fused_computation.79 | convolution fusion | flops 269221888 | bytes 4587520 | tf_op jit(solution)/shard_map/dot_general | solution.py:75
  129.1 9.3 %collective-permute-start.2 = (bf16[128,1024]{1,0:T(8,128)(2,1)S(1)}, bf16[128,1024]{1,0:T(8,128)(2,1)S(1)}, u32[]{:S(2)}, u32[]{:S(2)}) collective-permute-start(bf16[128,1024]{1,0:T(8,128)(2,1)S(1)} %pad_maximum_fusion.1), channel_id=1, source_target_pairs={{0,1},{1,2},{2,3},{3,0},{128,131},{129,128},{130,129},{131,130},{2... | collective-permute-start | bytes 786440 | tf_op jit(solution)/shard_map/ppermute | solution.py:52
  138.5 3.1 %fusion.142 = bf16[64,1024]{1,0:T(8,128)(2,1)S(1)} fusion(bf16[2,1024,1024]{2,1,0:T(8,128)(2,1)} %param.7, bf16[2,1024,1024]{2,1,0:T(8,128)(2,1)} %param.6, bf16[128,1024]{1,0:T(8,128)(2,1)S(1)} %collective-permute-done.5), kind=kOutput, calls=%fused_computation.97 | convolution fusion | flops 269221888 | bytes 4587520 | tf_op jit(solution)/shard_map/dot_general | solution.py:75
  141.6 2.8 %collective-permute-start.6 = (bf16[128,1024]{1,0:T(8,128)(2,1)S(1)}, bf16[128,1024]{1,0:T(8,128)(2,1)S(1)}, u32[]{:S(2)}, u32[]{:S(2)}) collective-permute-start(bf16[128,1024]{1,0:T(8,128)(2,1)S(1)} %pad_maximum_fusion.3), channel_id=1, source_target_pairs={{0,1},{1,2},{2,3},{3,0},{128,131},{129,128},{130,129},{131,130},{2... | collective-permute-start | bytes 786440 | tf_op jit(solution)/shard_map/ppermute | solution.py:52
  144.5 28.4 %collective-permute-done.2 = bf16[128,1024]{1,0:T(8,128)(2,1)S(1)} collective-permute-done((bf16[128,1024]{1,0:T(8,128)(2,1)S(1)}, bf16[128,1024]{1,0:T(8,128)(2,1)S(1)}, u32[]{:S(2)}, u32[]{:S(2)}) %collective-permute-start.2) | collective-permute-done | bytes 262176 | tf_op jit(solution)/shard_map/ppermute | solution.py:52
  172.9 3.1 %fusion.12 = f32[128,1024]{1,0:T(8,128)S(1)} fusion(bf16[2,1024,1024]{2,1,0:T(8,128)(2,1)} %param.7, bf16[2,1024,1024]{2,1,0:T(8,128)(2,1)} %param.6, bf16[64,1024]{1,0:T(8,128)(2,1)S(1)} %reshape_squeeze.6, bf16[64,1024]{1,0:T(8,128)(2,1)S(1)} %slice.83), kind=kOutput, calls=%fused_computation.12 | convolution fusion | flops 538574848 | bytes 4980736 | tf_op jit(solution)/shard_map/dot_general | solution.py:75
  176.0 4.0 %collective-permute-start.3 = (bf16[64,1024]{1,0:T(8,128)(2,1)S(1)}, bf16[64,1024]{1,0:T(8,128)(2,1)S(1)}, u32[]{:S(2)}, u32[]{:S(2)}) collective-permute-start(bf16[64,1024]{1,0:T(8,128)(2,1)S(1)} %fusion.149), channel_id=1, source_target_pairs={{0,1},{1,2},{2,3},{3,0},{128,131},{129,128},{130,129},{131,130},{2... | collective-permute-start | bytes 393224 | tf_op jit(solution)/shard_map/ppermute | solution.py:52
  180.0 3.1 %fusion = f32[128,1024]{1,0:T(8,128)S(1)} fusion(bf16[2,1024,1024]{2,1,0:T(8,128)(2,1)} %param.7, bf16[2,1024,1024]{2,1,0:T(8,128)(2,1)} %param.6, bf16[64,1024]{1,0:T(8,128)(2,1)S(1)} %reshape_squeeze.7, bf16[64,1024]{1,0:T(8,128)(2,1)S(1)} %slice.76), kind=kOutput, calls=%fused_computation | convolution fusion | flops 538574848 | bytes 4980736 | tf_op jit(solution)/shard_map/dot_general | solution.py:75
  183.1 10.4 %collective-permute-start.7 = (bf16[64,1024]{1,0:T(8,128)(2,1)S(1)}, bf16[64,1024]{1,0:T(8,128)(2,1)S(1)}, u32[]{:S(2)}, u32[]{:S(2)}) collective-permute-start(bf16[64,1024]{1,0:T(8,128)(2,1)S(1)} %fusion.147), channel_id=1, source_target_pairs={{0,1},{1,2},{2,3},{3,0},{128,131},{129,128},{130,129},{131,130},{2... | collective-permute-start | bytes 393224 | tf_op jit(solution)/shard_map/ppermute | solution.py:52
  193.5 3.9 %collective-permute-done.3 = bf16[64,1024]{1,0:T(8,128)(2,1)S(1)} collective-permute-done((bf16[64,1024]{1,0:T(8,128)(2,1)S(1)}, bf16[64,1024]{1,0:T(8,128)(2,1)S(1)}, u32[]{:S(2)}, u32[]{:S(2)}) %collective-permute-start.3) | collective-permute-done | bytes 131104 | tf_op jit(solution)/shard_map/ppermute | solution.py:52
  197.5 1.3 collective-permute-done.7
  198.9 0.3 pad_maximum_fusion.4
  199.3 25.0 %all_to_all.11 = bf16[32,2,2,1024]{3,2,1,0:T(2,128)(2,1)S(1)} all-to-all(bf16[32,2,2,1024]{3,2,1,0:T(2,128)(2,1)S(1)} %pad_maximum_fusion.4), channel_id=1, replica_groups={{0,4,8,12,16,20,24,28,32,36,40,44,48,52,56,60,64,68,72,76,80,84,88,92,9..., dimensions={0} | all-to-all | bytes 524288 | tf_op jit(solution)/shard_map/all_to_all | solution.py:66
  224.4 1.1 fusion.36
  (22 shorter events, 0.8 us)
Async XLA Ops:
  35.0 22.4 %collective-permute-start = (bf16[64,1024]{1,0:T(8,128)(2,1)S(1)}, bf16[64,1024]{1,0:T(8,128)(2,1)S(1)}, u32[]{:S(2)}, u32[]{:S(2)}) collective-permute-start(bf16[64,1024]{1,0:T(8,128)(2,1)S(1)} %reshape_squeeze.6), channel_id=1, source_target_pairs={{0,1},{1,2},{2,3},{3,0},{128,131},{129,128},{130,129},{131,130},{2... | collective-permute-start | bytes 393224 | tf_op jit(solution)/shard_map/ppermute | solution.py:52
  49.9 24.6 %collective-permute-start.4 = (bf16[64,1024]{1,0:T(8,128)(2,1)S(1)}, bf16[64,1024]{1,0:T(8,128)(2,1)S(1)}, u32[]{:S(2)}, u32[]{:S(2)}) collective-permute-start(bf16[64,1024]{1,0:T(8,128)(2,1)S(1)} %reshape_squeeze.7), channel_id=1, source_target_pairs={{0,1},{1,2},{2,3},{3,0},{128,131},{129,128},{130,129},{131,130},{2... | collective-permute-start | bytes 393224 | tf_op jit(solution)/shard_map/ppermute | solution.py:52
  60.6 65.4 %collective-permute-start.1 = (bf16[128,1024]{1,0:T(8,128)(2,1)S(1)}, bf16[128,1024]{1,0:T(8,128)(2,1)S(1)}, u32[]{:S(2)}, u32[]{:S(2)}) collective-permute-start(bf16[128,1024]{1,0:T(8,128)(2,1)S(1)} %pad_maximum_fusion), channel_id=1, source_target_pairs={{0,1},{1,2},{2,3},{3,0},{128,131},{129,128},{130,129},{131,130},{2... | collective-permute-start | bytes 786440 | tf_op jit(solution)/shard_map/ppermute | solution.py:52
  77.7 60.8 %collective-permute-start.5 = (bf16[128,1024]{1,0:T(8,128)(2,1)S(1)}, bf16[128,1024]{1,0:T(8,128)(2,1)S(1)}, u32[]{:S(2)}, u32[]{:S(2)}) collective-permute-start(bf16[128,1024]{1,0:T(8,128)(2,1)S(1)} %pad_maximum_fusion.2), channel_id=1, source_target_pairs={{0,1},{1,2},{2,3},{3,0},{128,131},{129,128},{130,129},{131,130},{2... | collective-permute-start | bytes 786440 | tf_op jit(solution)/shard_map/ppermute | solution.py:52
  129.1 43.7 %collective-permute-start.2 = (bf16[128,1024]{1,0:T(8,128)(2,1)S(1)}, bf16[128,1024]{1,0:T(8,128)(2,1)S(1)}, u32[]{:S(2)}, u32[]{:S(2)}) collective-permute-start(bf16[128,1024]{1,0:T(8,128)(2,1)S(1)} %pad_maximum_fusion.1), channel_id=1, source_target_pairs={{0,1},{1,2},{2,3},{3,0},{128,131},{129,128},{130,129},{131,130},{2... | collective-permute-start | bytes 786440 | tf_op jit(solution)/shard_map/ppermute | solution.py:52
  141.6 38.3 %collective-permute-start.6 = (bf16[128,1024]{1,0:T(8,128)(2,1)S(1)}, bf16[128,1024]{1,0:T(8,128)(2,1)S(1)}, u32[]{:S(2)}, u32[]{:S(2)}) collective-permute-start(bf16[128,1024]{1,0:T(8,128)(2,1)S(1)} %pad_maximum_fusion.3), channel_id=1, source_target_pairs={{0,1},{1,2},{2,3},{3,0},{128,131},{129,128},{130,129},{131,130},{2... | collective-permute-start | bytes 786440 | tf_op jit(solution)/shard_map/ppermute | solution.py:52
  176.0 21.4 %collective-permute-start.3 = (bf16[64,1024]{1,0:T(8,128)(2,1)S(1)}, bf16[64,1024]{1,0:T(8,128)(2,1)S(1)}, u32[]{:S(2)}, u32[]{:S(2)}) collective-permute-start(bf16[64,1024]{1,0:T(8,128)(2,1)S(1)} %fusion.149), channel_id=1, source_target_pairs={{0,1},{1,2},{2,3},{3,0},{128,131},{129,128},{130,129},{131,130},{2... | collective-permute-start | bytes 393224 | tf_op jit(solution)/shard_map/ppermute | solution.py:52
  183.1 15.7 %collective-permute-start.7 = (bf16[64,1024]{1,0:T(8,128)(2,1)S(1)}, bf16[64,1024]{1,0:T(8,128)(2,1)S(1)}, u32[]{:S(2)}, u32[]{:S(2)}) collective-permute-start(bf16[64,1024]{1,0:T(8,128)(2,1)S(1)} %fusion.147), channel_id=1, source_target_pairs={{0,1},{1,2},{2,3},{3,0},{128,131},{129,128},{130,129},{131,130},{2... | collective-permute-start | bytes 393224 | tf_op jit(solution)/shard_map/ppermute | solution.py:52
